TPU v7x, 32 devices: a whole 2x2x4 slice. The times are simulated.
32 devices in a mesh: dp: 8 (over y, x, core), tensor: 4 (over z).
Axes of the slice: x: 2, y: 2, z: 4, core: 2. Of those that a mesh axis runs over, the one named last changes fastest.
Arguments:
- hidden_in: float32 [8192, 1536], P(('dp', 'tensor')), may hold values from -6 to 6
- cotangent: float32 [8192, 1536], P(('dp', 'tensor')), may hold values from -6 to 6
- seq_lengths: int32 [8, 4], P('dp'), may hold values from 1 to 512, 1024 in all within a row
- query_weight: bfloat16 [1536, 1536], P('dp', 'tensor'), may hold values from -0.15625 to 0.15625
- key_weight: bfloat16 [1536, 768], P('dp', 'tensor'), may hold values from -0.15625 to 0.15625
- value_weight: bfloat16 [1536, 768], P('dp', 'tensor'), may hold values from -0.15625 to 0.15625
- output_weight: bfloat16 [1536, 1536], P('tensor', 'dp'), may hold values from -1.25 to 1.25
- w_gate: bfloat16 [1536, 4096], P('dp', 'tensor'), may hold values from -0.15625 to 0.15625
- w_up: bfloat16 [1536, 4096], P('dp', 'tensor'), may hold values from -0.15625 to 0.15625
- w_down: bfloat16 [4096, 1536], P('tensor', 'dp'), may hold values from -0.09375 to 0.09375
- gain_attn: bfloat16 [1536], P('dp'), may hold values from 0.099609375 to 1.8984375
- gain_mlp: bfloat16 [1536], P('dp'), may hold values from 0.099609375 to 1.8984375
Outputs:
- block_out: float32 [8192, 1536], P(('dp', 'tensor'))
- grad_input: float32 [8192, 1536], P(('dp', 'tensor'))
- grad_query: float32 [1536, 1536], P('dp', 'tensor')
- grad_key: float32 [1536, 768], P('dp', 'tensor')
- grad_value: float32 [1536, 768], P('dp', 'tensor')
- grad_output: float32 [1536, 1536], P('tensor', 'dp')
- grad_gate: float32 [1536, 4096], P('dp', 'tensor')
- grad_upproj: float32 [1536, 4096], P('dp', 'tensor')
- grad_down: float32 [4096, 1536], P('tensor', 'dp')
- grad_attnorm: float32 [1536], P('dp')
- grad_mlpnorm: float32 [1536], P('dp')
Inputs may be any that keep to these rules, and one draw needn't show every extreme that they name: `seq_lengths`: each row's lengths sum to 1024, and the longest of each row is exactly 512.
All inputs are finite; a program needn't handle non-finite values.
Results may differ from a plain program's by a relative error of at most 0.02.
Values may be sent and summed in bfloat16 or wider, within the bound.
No kernel may reach another device: no remote copies, remote signals or barrier semaphores. Data moves between devices by JAX's collectives and lax.ppermute only.
A program may use at most 128 MiB of HBM per device.

v0:
```python
import math

import jax
import jax.numpy as jnp
from jax import lax
from jax.sharding import PartitionSpec as P

QUERY_HEADS = 16
KEY_VALUE_HEADS = 8
HEAD_SIZE = 96


EPS = 1e-05
ROPE_BASE = 100000.0


def product(formula, left_side, right_side):
    return jnp.einsum(formula, left_side, right_side, preferred_element_type=jnp.float32)


def matrix_multiply(left_side, right_side):
    return jnp.dot(left_side, right_side, preferred_element_type=jnp.float32)


def multiply_by_transpose(left_side, right_side):
    return lax.dot_general(
        left_side, right_side, (((1,), (1,)), ((), ())), preferred_element_type=jnp.float32
    )


def transposed_times(left_side, right_side):
    return lax.dot_general(
        left_side, right_side, (((0,), (0,)), ((), ())), preferred_element_type=jnp.float32
    )


def positions_of(lengths_row, length_all):
    seq_ends = jnp.cumsum(lengths_row)
    seq_starts = seq_ends - lengths_row
    token_index = jnp.arange(length_all, dtype=jnp.int32)
    segment = jnp.sum((token_index[:, None] >= seq_ends[None, :]).astype(jnp.int32), axis=1)
    chosen = segment[:, None] == jnp.arange(lengths_row.shape[0], dtype=jnp.int32)[None, :]
    offsets = jnp.sum(jnp.where(chosen, seq_starts[None, :], 0), axis=1)
    return (segment, token_index - offsets)


def rope_tables(position, head_width):
    half_width = head_width // 2
    frequency = jnp.exp(
        -(2.0 * jnp.arange(half_width, dtype=jnp.float32) / head_width)
        * jnp.log(jnp.float32(ROPE_BASE))
    )
    angles = position.astype(jnp.float32)[:, None] * frequency[None, :]
    return (jnp.cos(angles), jnp.sin(angles))


def rotate_fwd(value_tensor, cosine, sine):
    half_width = value_tensor.shape[-1] // 2
    front_half = value_tensor[..., :half_width]
    back_half = value_tensor[..., half_width:]
    return jnp.concatenate(
        [front_half * cosine - back_half * sine, back_half * cosine + front_half * sine], axis=-1
    )


def inverse_rotation(value_tensor, cosine, sine):
    half_width = value_tensor.shape[-1] // 2
    front_half = value_tensor[..., :half_width]
    back_half = value_tensor[..., half_width:]
    return jnp.concatenate(
        [front_half * cosine + back_half * sine, back_half * cosine - front_half * sine], axis=-1
    )


def norm_forward(value_tensor, gain_vector):
    inverse = lax.rsqrt(jnp.mean(value_tensor * value_tensor, axis=-1, keepdims=True) + EPS)
    unit_rows = value_tensor * inverse
    return (unit_rows, inverse, (unit_rows * gain_vector.astype(jnp.float32)).astype(jnp.bfloat16))


def norm_backward(grad_normed, unit_rows, inverse, gain_vector):
    scaled = grad_normed * gain_vector.astype(jnp.float32)
    grad_gain = jnp.sum(grad_normed * unit_rows, axis=0)
    grad_rows = inverse * (
        scaled - unit_rows * jnp.mean(scaled * unit_rows, axis=-1, keepdims=True)
    )
    return (grad_rows, grad_gain)


def block_scores(query_block, key_rows, segment_block, index_block, segment, factor):
    scores = product("qkgd,skd->kgqs", query_block, key_rows) * factor
    length_all = key_rows.shape[0]
    allowed = (segment_block[:, None] == segment[None, :]) & (
        jnp.arange(length_all, dtype=jnp.int32)[None, :] <= index_block[:, None]
    )
    return jnp.where(allowed[None, None], scores, -jnp.inf)


def attend(queries, key_rows, value_row_block, segment, block_rows):
    length_all, kv_heads, query_group_width, head_width = queries.shape
    blocks = length_all // block_rows
    factor = 1.0 / math.sqrt(head_width)
    token_index = jnp.arange(length_all, dtype=jnp.int32)

    def per_block(pieces):
        query_block, segment_block, index_block = pieces
        scores = block_scores(query_block, key_rows, segment_block, index_block, segment, factor)
        maximum = jnp.max(scores, axis=-1, keepdims=True)
        logsum = maximum + jnp.log(jnp.sum(jnp.exp(scores - maximum), axis=-1, keepdims=True))
        weights = jnp.exp(scores - logsum).astype(jnp.bfloat16)
        mixed = product("kgqs,skd->qkgd", weights, value_row_block).astype(jnp.bfloat16)
        return (mixed, logsum[..., 0])

    mixed, logsum = lax.map(
        per_block,
        (
            queries.reshape(blocks, block_rows, kv_heads, query_group_width, head_width),
            segment.reshape(blocks, block_rows),
            token_index.reshape(blocks, block_rows),
        ),
    )
    return (mixed.reshape(length_all, kv_heads, query_group_width, head_width), logsum)


def attend_back(
    queries, key_rows, value_row_block, mixed, mixed_gradient, logsum, segment, block_rows
):
    length_all, kv_heads, query_group_width, head_width = queries.shape
    blocks = length_all // block_rows
    factor = 1.0 / math.sqrt(head_width)
    token_index = jnp.arange(length_all, dtype=jnp.int32)

    def per_block(carry, pieces):
        grad_keys, grad_values = carry
        query_block, mixed_block, grad_block, logsum_block, segment_block, index_block = pieces
        scores = block_scores(query_block, key_rows, segment_block, index_block, segment, factor)
        probability = jnp.exp(scores - logsum_block[..., None])
        grad_values = grad_values + product(
            "kgqs,qkgd->skd", probability.astype(jnp.bfloat16), grad_block
        )
        grad_probs = product("qkgd,skd->kgqs", grad_block, value_row_block)
        row_delta = jnp.sum(
            grad_block.astype(jnp.float32) * mixed_block.astype(jnp.float32), axis=-1
        )
        row_delta = jnp.transpose(row_delta, (1, 2, 0))[..., None]
        grad_scores = (probability * (grad_probs - row_delta) * factor).astype(jnp.bfloat16)
        grad_query = product("kgqs,skd->qkgd", grad_scores, key_rows)
        grad_keys = grad_keys + product("kgqs,qkgd->skd", grad_scores, query_block)
        return ((grad_keys, grad_values), grad_query)

    empty_grad = jnp.zeros((length_all, kv_heads, head_width), jnp.float32)
    shape_blocks = (blocks, block_rows, kv_heads, query_group_width, head_width)
    (grad_keys, grad_values), grad_query = lax.scan(
        per_block,
        (empty_grad, empty_grad),
        (
            queries.reshape(shape_blocks),
            mixed.reshape(shape_blocks),
            mixed_gradient.reshape(shape_blocks),
            logsum,
            segment.reshape(blocks, block_rows),
            token_index.reshape(blocks, block_rows),
        ),
    )
    return (
        grad_query.reshape(length_all, kv_heads, query_group_width, head_width),
        grad_keys,
        grad_values,
    )


def local(
    hidden_in,
    cotangent,
    seq_lengths,
    query_weight,
    key_weight,
    value_weight,
    output_weight,
    w_gate,
    w_up,
    w_down,
    gain_attn,
    gain_mlp,
):
    query_group_width = QUERY_HEADS // KEY_VALUE_HEADS
    gathered = (
        lax.all_gather(query_weight, "dp", axis=0, tiled=True),
        lax.all_gather(key_weight, "dp", axis=0, tiled=True),
        lax.all_gather(value_weight, "dp", axis=0, tiled=True),
        lax.all_gather(output_weight, "dp", axis=1, tiled=True),
        lax.all_gather(w_gate, "dp", axis=0, tiled=True),
        lax.all_gather(w_up, "dp", axis=0, tiled=True),
        lax.all_gather(w_down, "dp", axis=1, tiled=True),
        lax.all_gather(gain_attn, "dp", axis=0, tiled=True),
        lax.all_gather(gain_mlp, "dp", axis=0, tiled=True),
    )
    (
        query_full,
        key_full,
        value_full,
        output_full,
        gate_full,
        up_full,
        down_full,
        gain_one,
        gain_two,
    ) = gathered
    kv_local = key_full.shape[1] // HEAD_SIZE
    unit_one, inverse_one, normed_rows_one = norm_forward(hidden_in, gain_one)
    first_normalized = lax.all_gather(normed_rows_one, "tensor", axis=0, tiled=True)
    tok_rows = first_normalized.shape[0]
    block_rows = min(512, tok_rows)
    segment, position = positions_of(seq_lengths[0], tok_rows)
    cosine, sine = rope_tables(position, HEAD_SIZE)
    cos_heads, sin_heads = (cosine[:, None, None, :], sine[:, None, None, :])
    cosine_key_table, sine_key_table = (cosine[:, None, :], sine[:, None, :])
    unrotated_queries = matrix_multiply(first_normalized, query_full).reshape(
        tok_rows, kv_local, query_group_width, HEAD_SIZE
    )
    unrotated_keys = matrix_multiply(first_normalized, key_full).reshape(
        tok_rows, kv_local, HEAD_SIZE
    )
    value_row_block = (
        matrix_multiply(first_normalized, value_full)
        .astype(jnp.bfloat16)
        .reshape(tok_rows, kv_local, HEAD_SIZE)
    )
    query_rot = rotate_fwd(unrotated_queries, cos_heads, sin_heads).astype(jnp.bfloat16)
    key_rot = rotate_fwd(unrotated_keys, cosine_key_table, sine_key_table).astype(jnp.bfloat16)
    query_rot, key_rot, value_row_block = (query_rot, key_rot, value_row_block)
    mixed, logsum = attend(query_rot, key_rot, value_row_block, segment, block_rows)
    mixed_flat = mixed.reshape(tok_rows, -1)
    residual = hidden_in + lax.psum_scatter(
        matrix_multiply(mixed_flat, output_full), "tensor", scatter_dimension=0, tiled=True
    )
    unit_two, inverse_two, normed_rows_two = norm_forward(residual, gain_two)
    normed_two = lax.all_gather(normed_rows_two, "tensor", axis=0, tiled=True)
    gate_rows = matrix_multiply(normed_two, gate_full)
    up_rows = matrix_multiply(normed_two, up_full)
    sigmoid_gate = jax.nn.sigmoid(gate_rows)
    silu_gate = gate_rows * sigmoid_gate
    project_hidden_act = (silu_gate * up_rows).astype(jnp.bfloat16)
    gate_rows, up_rows, sigmoid_gate, silu_gate, hidden_act = (
        gate_rows,
        up_rows,
        sigmoid_gate,
        silu_gate,
        project_hidden_act,
    )
    block_out = residual + lax.psum_scatter(
        matrix_multiply(hidden_act, down_full).astype(jnp.bfloat16),
        "tensor",
        scatter_dimension=0,
        tiled=True,
    ).astype(jnp.float32)
    gathered = (
        lax.all_gather(query_weight, "dp", axis=0, tiled=True),
        lax.all_gather(key_weight, "dp", axis=0, tiled=True),
        lax.all_gather(value_weight, "dp", axis=0, tiled=True),
        lax.all_gather(output_weight, "dp", axis=1, tiled=True),
        lax.all_gather(w_gate, "dp", axis=0, tiled=True),
        lax.all_gather(w_up, "dp", axis=0, tiled=True),
        lax.all_gather(w_down, "dp", axis=1, tiled=True),
        lax.all_gather(gain_attn, "dp", axis=0, tiled=True),
        lax.all_gather(gain_mlp, "dp", axis=0, tiled=True),
    )
    (
        query_full,
        key_full,
        value_full,
        output_full,
        gate_full,
        up_full,
        down_full,
        gain_one,
        gain_two,
    ) = gathered
    cot_low = lax.all_gather(cotangent.astype(jnp.bfloat16), "tensor", axis=0, tiled=True)
    grad_act = multiply_by_transpose(cot_low, down_full)
    grad_down = transposed_times(hidden_act, cot_low)
    grad_gate_rows = (
        grad_act * up_rows * sigmoid_gate * (1.0 + gate_rows * (1.0 - sigmoid_gate))
    ).astype(jnp.bfloat16)
    grad_up_rows = (grad_act * silu_gate).astype(jnp.bfloat16)
    grad_gate = transposed_times(normed_two, grad_gate_rows)
    grad_upproj = transposed_times(normed_two, grad_up_rows)
    grad_normed_two = lax.psum_scatter(
        (
            multiply_by_transpose(grad_gate_rows, gate_full)
            + multiply_by_transpose(grad_up_rows, up_full)
        ).astype(jnp.bfloat16),
        "tensor",
        scatter_dimension=0,
        tiled=True,
    ).astype(jnp.float32)
    grad_middle, grad_gain_two = norm_backward(grad_normed_two, unit_two, inverse_two, gain_two)
    grad_resid = cotangent + grad_middle
    narrow_gradient = lax.all_gather(grad_resid.astype(jnp.bfloat16), "tensor", axis=0, tiled=True)
    grad_output = transposed_times(mixed_flat, narrow_gradient)
    mixed_gradient = (
        multiply_by_transpose(narrow_gradient, output_full)
        .astype(jnp.bfloat16)
        .reshape(tok_rows, kv_local, query_group_width, HEAD_SIZE)
    )
    grad_qrot, rotated_key_gradient, gradient_values_list = attend_back(
        query_rot, key_rot, value_row_block, mixed, mixed_gradient, logsum, segment, block_rows
    )
    grad_q = (
        inverse_rotation(grad_qrot, cos_heads, sin_heads).astype(jnp.bfloat16).reshape(tok_rows, -1)
    )
    key_gradient = (
        inverse_rotation(rotated_key_gradient, cosine_key_table, sine_key_table)
        .astype(jnp.bfloat16)
        .reshape(tok_rows, -1)
    )
    value_gradient = gradient_values_list.astype(jnp.bfloat16).reshape(tok_rows, -1)
    grad_query = transposed_times(first_normalized, grad_q)
    grad_key = transposed_times(first_normalized, key_gradient)
    grad_value = transposed_times(first_normalized, value_gradient)
    grad_normed_one = lax.psum_scatter(
        (
            multiply_by_transpose(grad_q, query_full)
            + multiply_by_transpose(key_gradient, key_full)
            + multiply_by_transpose(value_gradient, value_full)
        ).astype(jnp.bfloat16),
        "tensor",
        scatter_dimension=0,
        tiled=True,
    ).astype(jnp.float32)
    grad_first, grad_gain_one = norm_backward(grad_normed_one, unit_one, inverse_one, gain_one)
    grad_input = grad_resid + grad_first
    summed = (
        lax.psum_scatter(
            grad_query.astype(jnp.bfloat16), "dp", scatter_dimension=0, tiled=True
        ).astype(jnp.float32),
        lax.psum_scatter(
            grad_key.astype(jnp.bfloat16), "dp", scatter_dimension=0, tiled=True
        ).astype(jnp.float32),
        lax.psum_scatter(
            grad_value.astype(jnp.bfloat16), "dp", scatter_dimension=0, tiled=True
        ).astype(jnp.float32),
        lax.psum_scatter(
            grad_output.astype(jnp.bfloat16), "dp", scatter_dimension=1, tiled=True
        ).astype(jnp.float32),
        lax.psum_scatter(
            grad_gate.astype(jnp.bfloat16), "dp", scatter_dimension=0, tiled=True
        ).astype(jnp.float32),
        lax.psum_scatter(
            grad_upproj.astype(jnp.bfloat16), "dp", scatter_dimension=0, tiled=True
        ).astype(jnp.float32),
        lax.psum_scatter(
            grad_down.astype(jnp.bfloat16), "dp", scatter_dimension=1, tiled=True
        ).astype(jnp.float32),
        lax.psum_scatter(
            grad_gain_one.astype(jnp.bfloat16), "dp", scatter_dimension=0, tiled=True
        ).astype(jnp.float32),
        lax.psum_scatter(
            grad_gain_two.astype(jnp.bfloat16), "dp", scatter_dimension=0, tiled=True
        ).astype(jnp.float32),
    )
    output_grad = summed[3]
    gain_totals = lax.psum((summed[7], summed[8]), "tensor")
    return (
        block_out,
        grad_input,
        summed[0],
        summed[1],
        summed[2],
        output_grad,
        summed[4],
        summed[5],
        summed[6],
        gain_totals[0],
        gain_totals[1],
    )


def solution(mesh):
    in_specs = (
        P(("dp", "tensor"), None),
        P(("dp", "tensor"), None),
        P("dp", None),
        P("dp", "tensor"),
        P("dp", "tensor"),
        P("dp", "tensor"),
        P("tensor", "dp"),
        P("dp", "tensor"),
        P("dp", "tensor"),
        P("tensor", "dp"),
        P("dp"),
        P("dp"),
    )
    out_specs = (
        P(("dp", "tensor"), None),
        P(("dp", "tensor"), None),
        P("dp", "tensor"),
        P("dp", "tensor"),
        P("dp", "tensor"),
        P("tensor", "dp"),
        P("dp", "tensor"),
        P("dp", "tensor"),
        P("tensor", "dp"),
        P("dp"),
        P("dp"),
    )
    return jax.shard_map(local, mesh=mesh, in_specs=in_specs, out_specs=out_specs, check_vma=False)
```

profile of v0, /device:TPU:0, one launch (start us, length us, event | category | flops | bytes accessed | tf_op | source)
XLA Modules:
  0.0 1093.3 jit_solution(17131380025793593165)
XLA Ops:
  12.6 16.0 %all-reduce.6 = (bf16[1536]{0:T(1024)(128)(2,1)S(1)}, bf16[1536]{0:T(1024)(128)(2,1)}) all-reduce(bf16[1536]{0:T(1024)(128)(2,1)S(1)} %dynamic-update-slice, bf16[1536]{0:T(1024)(128)(2,1)S(1)} %dynamic-update-slice.1), channel_id=1, replica_groups=mesh['dp'=8,'tensor'=4] {'dp'}, use_global_device_ids=true, to_apply=%add | all-reduce | flops 3072 | bytes 12288
  56.3 37.9 %all-gather.10.cloned.1.call-done = bf16[1024,1536]{1,0:T(8,128)(2,1)} async-done(((bf16[256,1536]{1,0:T(8,128)(2,1)}), bf16[1024,1536]{1,0:T(8,128)(2,1)}) %all-gather.10.cloned.1.call-update) | async-done | bytes 3145744 | tf_op jit(solution)/shard_map/all_gather | solution.py:211
  98.4 20.2 %all-gather.12.cloned.1.call-done = bf16[1536,384]{1,0:T(8,128)(2,1)} async-done(((bf16[192,384]{1,0:T(8,128)(2,1)}), bf16[1536,384]{1,0:T(8,128)(2,1)}) %all-gather.12.cloned.1.call-update) | async-done | bytes 1179664 | tf_op jit(solution)/shard_map/all_gather | solution.py:188
  130.9 22.1 %while.27 = (s32[]{:T(128)}, bf16[2,512,2,2,96]{1,4,3,2,0:T(8,128)(2,1)}, f32[2,2,2,512]{3,2,1,0:T(2,128)}, s32[2,512]{1,0:T(2,128)}, s32[1024]{0:T(1024)S(1)}, ...) while((s32[]{:T(128)}, ...), condition=%wide.region_7.8_spmd, body=%wide.region_4.7_spmd.sunk | while | flops 830142464 | bytes 28917884 | solution.py:114
  161.9 110.3 %reduce-scatter.12.cloned.1.call-done = f32[256,1536]{1,0:T(8,128)} async-done(((f32[1024,1536]{1,0:T(8,128)}), f32[256,1536]{1,0:T(8,128)}) %reduce-scatter.12.cloned.1.call-update) | async-done | bytes 1572880 | tf_op jit(solution)/shard_map/reduce_scatter | solution.py:234
  279.2 27.5 %all-gather.20.cloned.1.call-done = bf16[1536,1024]{1,0:T(8,128)(2,1)} async-done(((bf16[192,1024]{1,0:T(8,128)(2,1)}), bf16[1536,1024]{1,0:T(8,128)(2,1)}) %all-gather.20.cloned.1.call-update) | async-done | bytes 3145744 | tf_op jit(solution)/shard_map/all_gather | solution.py:193
  306.6 65.5 %all-gather.16.cloned.1.call-done = bf16[1024,1536]{1,0:T(8,128)(2,1)} async-done(((bf16[256,1536]{1,0:T(8,128)(2,1)}), bf16[1024,1536]{1,0:T(8,128)(2,1)}) %all-gather.16.cloned.1.call-update) | async-done | bytes 3145744 | tf_op jit(solution)/shard_map/all_gather | solution.py:238
  380.4 24.5 %all-gather.18.cloned.1.call-done = bf16[1536,1024]{1,0:T(8,128)(2,1)} async-done(((bf16[192,1024]{1,0:T(8,128)(2,1)}), bf16[1536,1024]{1,0:T(8,128)(2,1)}) %all-gather.18.cloned.1.call-update) | async-done | bytes 3145744 | tf_op jit(solution)/shard_map/all_gather | solution.py:192
  413.1 57.4 %all-gather.24.cloned.1.call-done = bf16[1024,1536]{1,0:T(8,128)(2,1)} async-done(((bf16[256,1536]{1,0:T(8,128)(2,1)}), bf16[1024,1536]{1,0:T(8,128)(2,1)}) %all-gather.24.cloned.1.call-update) | async-done | bytes 3145744 | tf_op jit(solution)/shard_map/all_gather | solution.py:279
  470.5 32.7 %all-gather.22.cloned.1.call-done = bf16[1024,1536]{0,1:T(8,128)(2,1)} async-done(((bf16[1024,192]{0,1:T(8,128)(2,1)}), bf16[1024,1536]{0,1:T(8,128)(2,1)}) %all-gather.22.cloned.1.call-update) | async-done | bytes 3145744 | tf_op jit(solution)/shard_map/all_gather | solution.py:194
  523.5 60.5 %reduce-scatter.16.cloned.1.call-done = bf16[256,1536]{1,0:T(8,128)(2,1)} async-done(((bf16[1024,1536]{1,0:T(8,128)(2,1)}), bf16[256,1536]{1,0:T(8,128)(2,1)}) %reduce-scatter.16.cloned.1.call-update) | async-done | bytes 786448 | tf_op jit(solution)/shard_map/reduce_scatter | solution.py:288
  613.0 39.9 %all-gather.26.cloned.1.call-done = bf16[1024,1536]{1,0:T(8,128)(2,1)} async-done(((bf16[256,1536]{1,0:T(8,128)(2,1)}), bf16[1024,1536]{1,0:T(8,128)(2,1)}) %all-gather.26.cloned.1.call-update) | async-done | bytes 3145744 | tf_op jit(solution)/shard_map/all_gather | solution.py:299
  664.5 68.3 %while.28 = (s32[]{:T(128)}, f32[1024,2,96]{0,2,1:T(8,128)}, f32[1024,2,96]{0,2,1:T(8,128)}, f32[2,512,2,2,96]{1,0,4,3,2:T(2,128)}, bf16[2,512,2,2,96]{1,4,3,2,0...) while((s32[]{:T(128)}, f32[1024,2,96]{0,2,1:T(8,128)}, ...), condition=%wide.region_15.16_spmd.clone, body=%wide.region_13.15_spmd.clone.sunk | while | flops 2039478272 | bytes 50004156 | solution.py:153
  682.9 15.0 %dynamic_update_slice.20 = f32[2,512,2,2,96]{1,0,4,3,2:T(2,128)} dynamic-update-slice(f32[2,512,2,2,96]{1,0,4,3,2:T(2,128)} %get-tuple-element.535, f32[1,512,2,2,96]{1,0,4,3,2:T(1,128)S(1)} %copy.60, s32[]{:T(128)S(6)} %copy.79, s32[]{:T(128)} %constant.62.clone.1..sunk, s32[]{:T(128)} %constant.62.clone.1..sunk, s32[]{:T(128)} %constant.62.clone.1..sunk, s32[]{:T(128)} %constant.62.clone.1..sunk) | dynamic-update-slice | bytes 1572868 | tf_op jit(solution)/shard_map/while/body/jit(dynamic_update_index_in_dim)/dynamic_update_slice | solution.py:153
  717.8 15.0 %dynamic_update_slice.20 = f32[2,512,2,2,96]{1,0,4,3,2:T(2,128)} dynamic-update-slice(f32[2,512,2,2,96]{1,0,4,3,2:T(2,128)} %get-tuple-element.535, f32[1,512,2,2,96]{1,0,4,3,2:T(1,128)S(1)} %copy.60, s32[]{:T(128)S(6)} %copy.79, s32[]{:T(128)} %constant.62.clone.1..sunk, s32[]{:T(128)} %constant.62.clone.1..sunk, s32[]{:T(128)} %constant.62.clone.1..sunk, s32[]{:T(128)} %constant.62.clone.1..sunk) | dynamic-update-slice | bytes 1572868 | tf_op jit(solution)/shard_map/while/body/jit(dynamic_update_index_in_dim)/dynamic_update_slice | solution.py:153
  776.9 22.8 %reduce-scatter.28.cloned.1.call-done = bf16[192,1024]{1,0:T(8,128)(2,1)} async-done(((bf16[1536,1024]{1,0:T(8,128)(2,1)}), bf16[192,1024]{1,0:T(8,128)(2,1)}) %reduce-scatter.28.cloned.1.call-update) | async-done | bytes 393232 | tf_op jit(solution)/shard_map/reduce_scatter | solution.py:346
  801.6 36.0 %reduce-scatter.24.cloned.1.call-done = bf16[192,192]{1,0:T(8,128)(2,1)} async-done(((bf16[1536,192]{1,0:T(8,128)(2,1)}), bf16[192,192]{1,0:T(8,128)(2,1)}) %reduce-scatter.24.cloned.1.call-update) | async-done | bytes 73744 | tf_op jit(solution)/shard_map/reduce_scatter | solution.py:340
  839.2 36.4 %reduce-scatter.22.cloned.1.call-done = bf16[192,192]{1,0:T(8,128)(2,1)} async-done(((bf16[1536,192]{1,0:T(8,128)(2,1)}), bf16[192,192]{1,0:T(8,128)(2,1)}) %reduce-scatter.22.cloned.1.call-update) | async-done | bytes 73744 | tf_op jit(solution)/shard_map/reduce_scatter | solution.py:337
  877.2 38.8 %reduce-scatter.26.cloned.1.call-done = bf16[384,192]{0,1:T(8,128)(2,1)} async-done(((bf16[384,1536]{0,1:T(8,128)(2,1)}), bf16[384,192]{0,1:T(8,128)(2,1)}) %reduce-scatter.26.cloned.1.call-update) | async-done | bytes 147472 | tf_op jit(solution)/shard_map/reduce_scatter | solution.py:343
  917.6 38.7 %reduce-scatter.20.cloned.1.call-done = bf16[192,384]{1,0:T(8,128)(2,1)} async-done(((bf16[1536,384]{1,0:T(8,128)(2,1)}), bf16[192,384]{1,0:T(8,128)(2,1)}) %reduce-scatter.20.cloned.1.call-update) | async-done | bytes 147472 | tf_op jit(solution)/shard_map/reduce_scatter | solution.py:334
  958.0 61.1 %reduce-scatter.18.cloned.1.call-done = bf16[256,1536]{1,0:T(8,128)(2,1)} async-done(((bf16[1024,1536]{1,0:T(8,128)(2,1)}), bf16[256,1536]{1,0:T(8,128)(2,1)}) %reduce-scatter.18.cloned.1.call-update) | async-done | bytes 786448 | tf_op jit(solution)/shard_map/reduce_scatter | solution.py:321
  1020.8 13.5 %all-reduce.5 = (bf16[1536]{0:T(1024)(128)(2,1)S(1)}, bf16[1536]{0:T(1024)(128)(2,1)S(1)}) all-reduce(bf16[1536]{0:T(1024)(128)(2,1)S(1)} %get-tuple-element.256, bf16[1536]{0:T(1024)(128)(2,1)S(1)} %copy-done.32), channel_id=13, replica_groups=mesh['dp'=8,'tensor'=4] {'dp'}, use_global_device_ids=true, to_apply=%region_26.27.clone | all-reduce | flops 3072 | bytes 12288
  1034.4 12.1 %all-reduce.4 = (f32[192]{0:T(256)}, f32[192]{0:T(256)}) all-reduce(f32[192]{0:T(256)S(1)} %get-tuple-element.336, f32[192]{0:T(256)S(1)} %get-tuple-element.335), channel_id=1, replica_groups=mesh['dp'=8,'tensor'=4] {'tensor'}, use_global_device_ids=true, to_apply=%region_27.28 | all-reduce | flops 384 | bytes 3072 | tf_op jit(solution)/shard_map/psum | solution.py:363
  1046.5 35.3 %reduce-scatter.14.cloned.1.call-done = bf16[256,1536]{1,0:T(8,128)(2,1)} async-done(((bf16[1024,1536]{1,0:T(8,128)(2,1)}), bf16[256,1536]{1,0:T(8,128)(2,1)}) %reduce-scatter.14.cloned.1.call-update) | async-done | bytes 786448 | tf_op jit(solution)/shard_map/reduce_scatter | solution.py:251
  (239 shorter events, 259.5 us)
Async XLA Ops:
  7.2 87.0 %all-gather.10.cloned.1.call-start = ((), (), s32[]{:S(2)}) async-start(), calls=%async_computation.11 | async-start | bytes 3932160 | tf_op jit(solution)/shard_map/all_gather | solution.py:211
  31.2 87.4 %all-gather.12.cloned.1.call-start = ((), (), s32[]{:S(2)}) async-start(), calls=%async_computation.12 | async-start | bytes 1327104 | tf_op jit(solution)/shard_map/all_gather | solution.py:188
  31.9 123.2 %all-gather.14.cloned.1.call-start = ((), (), s32[]{:S(2)}) async-start(), calls=%async_computation.13 | async-start | bytes 1327104 | tf_op jit(solution)/shard_map/all_gather | solution.py:191
  32.7 239.5 %reduce-scatter.12.cloned.1.call-start = ((), (), s32[]{:S(2)}) async-start(), calls=%async_computation.14 | async-start | bytes 7864320 | tf_op jit(solution)/shard_map/reduce_scatter | solution.py:234
  161.2 145.4 %all-gather.20.cloned.1.call-start = ((), (), s32[]{:S(2)}) async-start(), calls=%async_computation.17 | async-start | bytes 3538944 | tf_op jit(solution)/shard_map/all_gather | solution.py:193
  161.8 210.3 %all-gather.16.cloned.1.call-start = ((), (), s32[]{:S(2)}) async-start(), calls=%async_computation.15 | async-start | bytes 3932160 | tf_op jit(solution)/shard_map/all_gather | solution.py:238
  276.1 128.8 %all-gather.18.cloned.1.call-start = ((), (), s32[]{:S(2)}) async-start(), calls=%async_computation.16 | async-start | bytes 3538944 | tf_op jit(solution)/shard_map/all_gather | solution.py:192
  276.8 193.6 %all-gather.24.cloned.1.call-start = ((), (), s32[]{:S(2)}) async-start(), calls=%async_computation.20 | async-start | bytes 3932160 | tf_op jit(solution)/shard_map/all_gather | solution.py:279
  277.9 225.3 %all-gather.22.cloned.1.call-start = ((), (), s32[]{:S(2)}) async-start(), calls=%async_computation.18 | async-start | bytes 3538944 | tf_op jit(solution)/shard_map/all_gather | solution.py:194
  278.6 305.4 %reduce-scatter.16.cloned.1.call-start = ((), (), s32[]{:S(2)}) async-start(), calls=%async_computation.21 | async-start | bytes 3932160 | tf_op jit(solution)/shard_map/reduce_scatter | solution.py:288
  523.4 129.4 %all-gather.26.cloned.1.call-start = ((), (), s32[]{:S(2)}) async-start(), calls=%async_computation.22 | async-start | bytes 3932160 | tf_op jit(solution)/shard_map/all_gather | solution.py:299
  589.4 183.5 %reduce-scatter.32.cloned.1.call-start = ((), (), s32[]{:S(2)}) async-start(), calls=%async_computation.30 | async-start | bytes 3538944 | tf_op jit(solution)/shard_map/reduce_scatter | solution.py:352
  597.1 177.8 %reduce-scatter.30.cloned.1.call-start = ((), (), s32[]{:S(2)}) async-start(), calls=%async_computation.29 | async-start | bytes 3538944 | tf_op jit(solution)/shard_map/reduce_scatter | solution.py:349
  605.1 194.5 %reduce-scatter.28.cloned.1.call-start = ((), (), s32[]{:S(2)}) async-start(), calls=%async_computation.28 | async-start | bytes 3538944 | tf_op jit(solution)/shard_map/reduce_scatter | solution.py:346
  612.9 224.7 %reduce-scatter.24.cloned.1.call-start = ((), (), s32[]{:S(2)}) async-start(), calls=%async_computation.26 | async-start | bytes 884736 | tf_op jit(solution)/shard_map/reduce_scatter | solution.py:340
  738.8 136.9 %reduce-scatter.22.cloned.1.call-start = ((), (), s32[]{:S(2)}) async-start(), calls=%async_computation.25 | async-start | bytes 884736 | tf_op jit(solution)/shard_map/reduce_scatter | solution.py:337
  745.5 170.5 %reduce-scatter.26.cloned.1.call-start = ((), (), s32[]{:S(2)}) async-start(), calls=%async_computation.27 | async-start | bytes 1327104 | tf_op jit(solution)/shard_map/reduce_scatter | solution.py:343
  750.3 206.0 %reduce-scatter.20.cloned.1.call-start = ((), (), s32[]{:S(2)}) async-start(), calls=%async_computation.24 | async-start | bytes 1327104 | tf_op jit(solution)/shard_map/reduce_scatter | solution.py:334
  757.8 261.3 %reduce-scatter.18.cloned.1.call-start = ((), (), s32[]{:S(2)}) async-start(), calls=%async_computation.23 | async-start | bytes 3932160 | tf_op jit(solution)/shard_map/reduce_scatter | solution.py:321
  763.9 317.9 %reduce-scatter.14.cloned.1.call-start = ((), (), s32[]{:S(2)}) async-start(), calls=%async_computation.19 | async-start | bytes 3932160 | tf_op jit(solution)/shard_map/reduce_scatter | solution.py:251
  772.1 246.9 %copy-start.1 = (f32[256,1536]{1,0:T(8,128)S(1)}, f32[256,1536]{1,0:T(8,128)}, u32[]{:S(2)}) copy-start(f32[256,1536]{1,0:T(8,128)} %param.16) | copy-start | bytes 4718596
  772.1 246.9 %copy-start.25 = (f32[1536]{0:T(1024)S(1)}, f32[1536]{0:T(1024)}, u32[]{:S(2)}) copy-start(f32[1536]{0:T(1024)} %copy-done.24) | copy-start | bytes 18436
  774.9 306.9 %copy-start.29 = (f32[256]{0:T(256)S(1)}, f32[256]{0:T(256)}, u32[]{:S(2)}) copy-start(f32[256]{0:T(256)} %copy-done.28) | copy-start | bytes 3076
  774.9 306.9 %copy-start.34 = (f32[256]{0:T(256)S(1)}, f32[256]{0:T(256)}, u32[]{:S(2)}) copy-start(f32[256]{0:T(256)} %copy-done.33) | copy-start | bytes 3076
  (37 other events, 1182.6 us)
Sparse Core Ops, SparseCore 0:
  31.3 62.7 all-gather.9
  96.0 22.5 all-gather.11
  120.5 23.9 all-gather.13
  161.4 110.7 reduce-scatter.11
  273.9 32.6 all-gather.19
  308.6 63.4 all-gather.15
  374.0 30.8 all-gather.17
  407.0 63.4 all-gather.23
  472.4 30.8 all-gather.21
  523.6 60.3 reduce-scatter.15
  589.5 63.3 all-gather.25
  656.1 44.6 reduce-scatter.31
  704.2 46.0 reduce-scatter.29
  753.6 46.0 reduce-scatter.27
  802.7 34.9 reduce-scatter.23
  840.6 34.9 reduce-scatter.21
  879.3 36.6 reduce-scatter.25
  919.6 36.6 reduce-scatter.19
  958.6 60.3 reduce-scatter.17
  1021.2 60.5 reduce-scatter.13
where the time goes:
time: 1100 us; the launch traced here: 1090 us
  waiting for transfers between devices  749 us (68%)
  matrix products  152 us (14%)
  blocking collectives  63.4 us (6%)
  local copies, waits for them, and re-layouts  60.7 us (6%)
  other arithmetic  49.9 us (5%)
  between operations  16.5 us (2%)
    reduce_scatter x1, waiting for transfers between devices, local(): lax.psum_scatter(matrix_multiply(mixed_flat, output_full), 'tensor', scat...  110 us
    all_gather x1, waiting for transfers between devices, local(): normed_two = lax.all_gather(normed_rows_two, 'tensor', axis=0, tiled=True)  65.5 us
    reduce_scatter x1, waiting for transfers between devices, local(): lax.psum_scatter((multiply_by_transpose(grad_q, query_full) + multiply_by...  61.1 us
    reduce_scatter x1, waiting for transfers between devices, local(): lax.psum_scatter((multiply_by_transpose(grad_gate_rows, gate_full) + mult...  60.5 us
    all_gather x1, waiting for transfers between devices, local(): lax.all_gather(cotangent.astype(jnp.bfloat16), 'tensor', axis=0, tiled=True)  57.4 us
    dot_general x14, matrix products, product(): jnp.einsum(formula, left_side, right_side, preferred_element_type=jnp.flo...  43.7 us
    all_gather x1, waiting for transfers between devices, local(): lax.all_gather(grad_resid.astype(jnp.bfloat16), 'tensor', axis=0, tiled=T...  39.9 us
    dot_general x7, matrix products, transposed_times(): lax.dot_general(left_side, right_side, (((0,), (0,)), ((), ())), preferre...  39 us
  transfers between devices with their start and end apart: 20, of which 17 were waited for; matrix products, arithmetic and copies ran while one was open for 20% of the time, Pallas kernels for 0%

commit v1 on v0

--- a/solution.py
+++ b/solution.py
@@ -3,6 +3,8 @@
 import jax
 import jax.numpy as jnp
 from jax import lax
+from jax.experimental import pallas as pl
+from jax.experimental.pallas import tpu as pltpu
 from jax.sharding import PartitionSpec as P
 
 QUERY_HEADS = 16
@@ -169,7 +171,7 @@
     )
 
 
-def local(
+def local_plain(
     hidden_in,
     cotangent,
     seq_lengths,
@@ -376,7 +378,784 @@
     )
 
 
+BF = jnp.bfloat16
+F32 = jnp.float32
+NEG = -1e30
+VMEM_LIMIT = 60 * 1024 * 1024
+
+
+def dot_nn(a, b):
+    return lax.dot_general(a, b, (((1,), (0,)), ((), ())), preferred_element_type=F32)
+
+
+def dot_nt(a, b):
+    return lax.dot_general(a, b, (((1,), (1,)), ((), ())), preferred_element_type=F32)
+
+
+def dot_tn(a, b):
+    return lax.dot_general(a, b, (((0,), (0,)), ((), ())), preferred_element_type=F32)
+
+
+def whole(shape):
+    zeros = (0,) * len(shape)
+    return pl.BlockSpec(tuple(shape), lambda *_: zeros)
+
+
+def call(kernel, name, grid, ins, outs, scalars=(), scratch=(), flops=0):
+    moved = sum(a.size * a.dtype.itemsize for a, _ in ins)
+    moved += sum(math.prod(s) * jnp.dtype(d).itemsize for s, d, _ in outs)
+    return pl.pallas_call(
+        kernel,
+        name=name,
+        out_shape=[jax.ShapeDtypeStruct(s, d) for s, d, _ in outs],
+        grid_spec=pltpu.PrefetchScalarGridSpec(
+            num_scalar_prefetch=len(scalars),
+            grid=grid,
+            in_specs=[s for _, s in ins],
+            out_specs=[s for _, _, s in outs],
+            scratch_shapes=list(scratch),
+        ),
+        compiler_params=pltpu.CompilerParams(
+            dimension_semantics=("arbitrary",) * len(grid), vmem_limit_bytes=VMEM_LIMIT
+        ),
+        cost_estimate=pl.CostEstimate(flops=int(flops), bytes_accessed=int(moved), transcendentals=0),
+    )(*scalars, *[a for a, _ in ins])
+
+
+def swap_core(x):
+    return lax.ppermute(x, "dp", [(i, i ^ 1) for i in range(8)])
+
+
+def swap_p(x, k):
+    return lax.ppermute(x, "dp", [(i, i ^ (2 * k)) for i in range(8)])
+
+
+def swap_t(x, k):
+    return lax.ppermute(x, "tensor", [(i, i ^ k) for i in range(4)])
+
+
+def shift_up(x):
+    return lax.ppermute(x, "tensor", [(i, i + 1) for i in range(3)])
+
+
+def shift_down(x):
+    return lax.ppermute(x, "tensor", [(i + 1, i) for i in range(3)])
+
+
+def gather_p(x):
+    h = x.shape[0] // 2
+    one = swap_p(x, 1)
+    two = swap_p(x, 2)
+    return (x, one, two, swap_p(one[:h], 2), swap_p(two[h:], 1))
+
+
+def reduce_p(a, b):
+    ya = swap_p(a[3], 2)
+    xb = swap_p(b[3], 1)
+    x1b = swap_p(b[1], 1)
+    y2a = swap_p(a[2], 2)
+    x1a = swap_p(a[1] + ya, 1)
+    y2b = swap_p(b[2] + xb, 2)
+    return (
+        [(a[0], x1a, y2a), (b[0], x1b, y2b)]
+    )
+
+
+def added(parts, at=None):
+    total = None
+    for part in parts:
+        value = (part if at is None else part[at]).astype(F32)
+        total = value if total is None else total + value
+    return total
+
+
+def four(array, rows, width):
+    return [
+        (array, pl.BlockSpec((rows, width), lambda i, s, r=r: (i, s[0] ^ r))) for r in range(4)
+    ]
+
+
+def cast_kernel(s, a0, a1, a2, a3, out):
+    w = a0.shape[1]
+    for r, a in enumerate((a0, a1, a2, a3)):
+        out[:, r * w : (r + 1) * w] = a[...].astype(BF)
+
+
+def norm_one_kernel(s, a0, a1, a2, a3, gain, out):
+    x = jnp.concatenate([a0[...], a1[...], a2[...], a3[...]], axis=1)
+    inv = lax.rsqrt(jnp.mean(x * x, axis=1, keepdims=True) + EPS)
+    out[...] = (x * inv * gain[...]).astype(BF)
+
+
+def norm_two_kernel(s, a0, a1, a2, a3, own, recv, gain, resid, out):
+    x = jnp.concatenate([a0[...], a1[...], a2[...], a3[...]], axis=1)
+    x = x + own[...] + recv[...].astype(F32)
+    resid[...] = x
+    inv = lax.rsqrt(jnp.mean(x * x, axis=1, keepdims=True) + EPS)
+    out[...] = (x * inv * gain[...]).astype(BF)
+
+
+def back_two_kernel(s, c0, c1, c2, c3, keep, recv, far, resid, gain, grad, low, gsum):
+    cot = jnp.concatenate([c0[...], c1[...], c2[...], c3[...]], axis=1)
+    dn = keep[0].astype(F32) + recv[0].astype(F32) + far[...].astype(F32)
+    x = resid[...]
+    inv = lax.rsqrt(jnp.mean(x * x, axis=1, keepdims=True) + EPS)
+    unit = x * inv
+    scaled = dn * gain[...]
+    value = cot + inv * (scaled - unit * jnp.mean(scaled * unit, axis=1, keepdims=True))
+    grad[...] = value
+    low[...] = value.astype(BF)
+
+    @pl.when(pl.program_id(0) == 0)
+    def _():
+        gsum[...] = jnp.zeros_like(gsum)
+
+    gsum[...] += jnp.sum(dn * unit, axis=0, keepdims=True)
+
+
+def back_one_kernel(s, a0, a1, a2, a3, own, recv, grad, gain, out, gsum):
+    x = jnp.concatenate([a0[...], a1[...], a2[...], a3[...]], axis=1)
+    dn = own[...] + recv[...].astype(F32)
+    inv = lax.rsqrt(jnp.mean(x * x, axis=1, keepdims=True) + EPS)
+    unit = x * inv
+    scaled = dn * gain[...]
+    value = grad[...] + inv * (scaled - unit * jnp.mean(scaled * unit, axis=1, keepdims=True))
+    store_natural(s, out, value)
+
+    @pl.when(pl.program_id(0) == 0)
+    def _():
+        gsum[...] = jnp.zeros_like(gsum)
+
+    gsum[...] += jnp.sum(dn * unit, axis=0, keepdims=True)
+
+
+def store_natural(s, out, value):
+    w = out.shape[1] // 4
+    for r in range(4):
+        at = pl.multiple_of((s[0] ^ r) * w, 128)
+        out[:, pl.ds(at, w)] = value[:, r * w : (r + 1) * w]
+
+
+def block_out_kernel(s, resid, keep, recv, far, out):
+    value = resid[...] + keep[0].astype(F32) + recv[0].astype(F32) + far[...].astype(F32)
+    store_natural(s, out, value)
+
+
+def pack_kernel(s, q, k, v, o, keep_a, send_a, keep_o, send_o):
+    def half(ref, h):
+        n = ref.shape[1] // 2
+        return ref[:, h * n : (h + 1) * n]
+
+    for core in range(2):
+
+        @pl.when(s[0] == core)
+        def _(core=core):
+            for a_out, o_out, h in ((keep_a, keep_o, core), (send_a, send_o, 1 - core)):
+                a_out[...] = jnp.concatenate([half(q, h), half(k, h), half(v, h)], axis=1)
+                n = o.shape[0] // 2
+                o_out[...] = o[h * n : (h + 1) * n, :]
+
+
+def rotated(x, cosine, sine):
+    n = x.shape[1] // 2
+    return x * cosine + jnp.concatenate([x[:, n:], x[:, :n]], axis=1) * sine
+
+
+def rotated_back(x, cosine, sine):
+    n = x.shape[1] // 2
+    return x * cosine - jnp.concatenate([x[:, n:], x[:, :n]], axis=1) * sine
+
+
+def allowed_of(s, lens, b, rows, keys):
+    query_at = s[2] + lax.broadcasted_iota(jnp.int32, (rows, 1), 0)
+    start = jnp.zeros((rows, 1), jnp.int32)
+    end = jnp.int32(0)
+    for i in range(lens.shape[1]):
+        end = end + lens[b, i]
+        start = start + jnp.where(query_at >= end, lens[b, i], 0)
+    key_at = s[2] - (keys - rows) + lax.broadcasted_iota(jnp.int32, (rows, keys), 1)
+    return (key_at <= query_at) & (key_at >= start)
+
+
+def pick(j, half, top, bottom):
+    return jnp.where(j < half, top, bottom)
+
+
+def attention_kernel(
+    s, lens, x0, x0p, x1, x1p, x2, x2p, w0, w1, w2, w3t, w3b, cos, sin, q_out, k_out, v_out, o_out, l_out
+):
+    j = pl.program_id(0)
+    e = HEAD_SIZE
+    w = jnp.concatenate([w0[0], w1[0], w2[0], pick(j, 2, w3t[0], w3b[0])], axis=0)
+    factor = 1.0 / math.sqrt(e)
+    rows = x0.shape[0]
+    keys = 3 * rows
+    for b, (own, near, far) in enumerate(((x0, x1, x2), (x0p, x1p, x2p))):
+        y = dot_nn(own[...], w)
+        halo = jnp.concatenate([far[...], near[...]], axis=0)
+        z = dot_nn(halo, w[:, 128:])
+        cosine, sine = cos[b], sin[b]
+        k = jnp.concatenate([z[:, 2 * e - 128 : 3 * e - 128], y[:, 2 * e : 3 * e]], axis=0)
+        k = rotated(k, cosine, sine).astype(BF)
+        v = jnp.concatenate([z[:, 3 * e - 128 :], y[:, 3 * e :]], axis=0).astype(BF)
+        k_out[0, b] = k
+        v_out[0, b] = v
+        allowed = allowed_of(s, lens, b, rows, keys)
+        mixed = []
+        for h in range(2):
+            q = rotated(y[:, h * e : (h + 1) * e], cosine[keys - rows :], sine[keys - rows :])
+            q = q.astype(BF)
+            q_out[0, b, h] = q
+            score = jnp.where(allowed, dot_nt(q, k) * factor, NEG)
+            top = jnp.max(score, axis=1, keepdims=True)
+            weight = jnp.exp(score - top)
+            total = jnp.sum(weight, axis=1, keepdims=True)
+            l_out[0, b, h] = top + jnp.log(total)
+            mixed.append(dot_nn(weight.astype(BF), v) / total)
+        o_out[0, b] = jnp.concatenate(mixed, axis=1).astype(BF)
+
+
+def joined_heads(o):
+    return jnp.concatenate([o[j] for j in range(4)], axis=1)
+
+
+def project_kernel(o, w0, w1, w2, w3t, w3b, own, send):
+    rows = o.shape[2]
+    n = w0.shape[2]
+    ws = [w[...].reshape(-1, n) for w in (w0, w1, w2)]
+    ws.append(jnp.concatenate([w3t[...], w3b[...]], axis=0).reshape(-1, n))
+    for b, out in ((1, send), (0, own)):
+        mixed = jnp.concatenate([o[j, b] for j in range(4)], axis=1)
+        for r in range(4):
+            out[:, r * n : (r + 1) * n] = dot_nn(mixed, ws[r]).astype(out.dtype)
+
+
+def attention_back_kernel(
+    s, lens, n0, n1, w0, w1, w2, w3, q_in, k_in, v_in, o_in, l_in, cos, sin, d_own, d_near, d_far
+):
+    e = HEAD_SIZE
+    factor = 1.0 / math.sqrt(e)
+    rows = n0.shape[0]
+    keys = 3 * rows
+    w = jnp.concatenate([w0[0], w1[0], w2[0], w3[0]], axis=1)
+    for b, low in enumerate((n0, n1)):
+        datt = dot_nt(low[...], w).astype(BF)
+        product = datt.astype(F32) * o_in[0, b].astype(F32)
+        k, v = k_in[0, b], v_in[0, b]
+        cosine, sine = cos[b], sin[b]
+        allowed = allowed_of(s, lens, b, rows, keys)
+        dk = jnp.zeros((keys, e), F32)
+        dv = jnp.zeros((keys, e), F32)
+        dq = []
+        for h in range(2):
+            q = q_in[0, b, h]
+            da = datt[:, h * e : (h + 1) * e]
+            delta = jnp.sum(product[:, h * e : (h + 1) * e], axis=1, keepdims=True)
+            score = jnp.where(allowed, dot_nt(q, k) * factor, NEG)
+            prob = jnp.exp(score - l_in[0, b, h])
+            dscore = (prob * (dot_nt(da, v) - delta) * factor).astype(BF)
+            dv = dv + dot_tn(prob.astype(BF), da)
+            dk = dk + dot_tn(dscore, q)
+            dq.append(rotated_back(dot_nn(dscore, k), cosine[keys - rows :], sine[keys - rows :]))
+        dk = rotated_back(dk, cosine, sine)
+        own = slice(keys - rows, keys)
+        d_own[0, b] = jnp.concatenate([dq[0], dq[1], dk[own], dv[own]], axis=1).astype(BF)
+        pad = jnp.zeros((rows, 2 * e - 128), F32)
+        for out, at in ((d_far, slice(0, rows)), (d_near, slice(rows, 2 * rows))):
+            out[0, b] = jnp.concatenate([pad, dk[at], dv[at]], axis=1).astype(BF)
+
+
+def attention_grad_kernel(x0, x0p, x1, x1p, x2, x2p, d_own, d_near, d_far, g0, g1, g2, g3, xt):
+    m = x0.shape[0]
+
+    @pl.when(pl.program_id(0) == 0)
+    def _():
+        for i, x in enumerate((x0, x0p, x1, x1p, x2, x2p)):
+            xt[:, i * m : (i + 1) * m] = x[...].T
+
+    own = dot_nn(xt[:, : 2 * m], d_own[0].reshape(2 * m, -1))
+    halo = jnp.concatenate([d_near[0].reshape(2 * m, -1), d_far[0].reshape(2 * m, -1)], axis=0)
+    other = dot_nn(xt[:, 2 * m :], halo)
+    total = jnp.concatenate([own[:, :128], own[:, 128:] + other], axis=1).astype(BF)
+    n = g0.shape[1]
+    for r, g in enumerate((g0, g1, g2, g3)):
+        g[0] = total[r * n : (r + 1) * n]
+
+
+def output_grad_kernel(n0, n1, o, g0a, g0b, g1a, g1b, g2a, g2b, g3a, g3b):
+    n = g0a.shape[2]
+    low = jnp.concatenate([n0[...], n1[...]], axis=0)
+    for j in range(4):
+        mixed = o[j].reshape(low.shape[0], -1)
+        total = dot_tn(mixed, low).astype(BF)
+        outs = (g0a, g1a, g2a, g3a) if j < 2 else (g0b, g1b, g2b, g3b)
+        for r, g in enumerate(outs):
+            g[j % 2] = total[:, r * n : (r + 1) * n]
+
+
+def inner_back_kernel(d_own, s_near, w0, w1, w2, w3t, w3b, own, send):
+    m = d_own.shape[2]
+    ws = [[w[j] for j in range(4)] for w in (w0, w1, w2)]
+    ws.append([w3t[0], w3t[1], w3b[0], w3b[1]])
+    n = w0.shape[1]
+    for b, out in ((1, send), (0, own)):
+        ds = []
+        for j in range(4):
+            d = d_own[j, b]
+            extra = d[:, 128:].astype(F32) + s_near[j, b].astype(F32)
+            ds += [d[:, :128], extra.astype(BF)]
+        d = jnp.concatenate(ds, axis=1)
+        for r in range(4):
+            out[:, r * n : (r + 1) * n] = dot_nt(d, jnp.concatenate(ws[r], axis=1)).astype(out.dtype)
+
+
+def hidden_kernel(
+    x0, x1, x2, x3, c0, c1, c2, c3, a0, a1, a2, a3t, a3b, d0, d1, d2, d3t, d3b, z_out
+):
+    q = pl.program_id(0)
+    x = jnp.concatenate([x0[...], x1[...], x2[...], x3[...]], axis=0)
+    cot = jnp.concatenate([c0[...], c1[...], c2[...], c3[...]], axis=0)
+
+    def weight(i):
+        return jnp.concatenate([a0[i], a1[i], a2[i], pick(q, 1, a3t[i], a3b[i])], axis=0)
+
+    gate = dot_nn(x, weight(0))
+    up = dot_nn(x, weight(1))
+    down = jnp.concatenate([d0[0], d1[0], d2[0], pick(q, 1, d3t[0], d3b[0])], axis=0)
+    dact = dot_nn(cot, down)
+    sig = 1.0 / (1.0 + jnp.exp(-gate))
+    silu = gate * sig
+    z_out[0, 0] = (dact * up * sig * (1.0 + gate * (1.0 - sig))).astype(BF)
+    z_out[1, 0] = (dact * silu).astype(BF)
+    z_out[2, 0] = (silu * up).astype(BF)
+
+
+def hidden_back_kernel(count, z, w0, w1, w2, w3t, w3b, send, keep):
+    i = pl.program_id(0)
+    n = w0.shape[1]
+    lhs, ws = [], [[], [], [], []]
+    for q in range(2):
+        for m in range(count):
+            lhs.append(z[m, q])
+            for r, w in enumerate((w0, w1, w2)):
+                ws[r].append(w[q * count + m])
+            ws[3].append((w3t, w3b)[q][m])
+    lhs = jnp.concatenate(lhs, axis=1)
+    parts = [dot_nt(lhs, jnp.concatenate(w, axis=1)).astype(BF) for w in ws]
+
+    @pl.when(i < 2)
+    def _():
+        for r in range(4):
+            send[0, :, r * n : (r + 1) * n] = parts[r]
+
+    @pl.when(i >= 2)
+    def _():
+        for r in range(4):
+            keep[0, :, r * n : (r + 1) * n] = parts[r]
+
+
+def hidden_grad_kernel(x0, x1, x2, x3, c0, c1, c2, c3, z, g0, g1, g2, g3, xt):
+    m = pl.program_id(0)
+    rows = x0.shape[0]
+
+    @pl.when(m == 0)
+    def _():
+        for i, x in enumerate((x0, x1, x2, x3)):
+            xt[:, i * rows : (i + 1) * rows] = x[...].T
+
+    @pl.when(m == 2)
+    def _():
+        for i, x in enumerate((c0, c1, c2, c3)):
+            xt[:, i * rows : (i + 1) * rows] = x[...].T
+
+    total = dot_nn(xt[...], z[0, 0]).astype(BF)
+    n = g0.shape[1]
+    for r, g in enumerate((g0, g1, g2, g3)):
+        g[0] = total[r * n : (r + 1) * n]
+
+
+def local_fast(
+    hidden_in,
+    cotangent,
+    seq_lengths,
+    query_weight,
+    key_weight,
+    value_weight,
+    output_weight,
+    w_gate,
+    w_up,
+    w_down,
+    gain_attn,
+    gain_mlp,
+):
+    plane = lax.axis_index("dp") // 2
+    core = lax.axis_index("dp") % 2
+    level = lax.axis_index("tensor")
+    first = core == 0
+    rows, width = hidden_in.shape
+    quarter = width // 4
+    shard = quarter // 2
+    sp = jnp.stack([plane, core, level * rows]).astype(jnp.int32)
+    sc = sp[1:2]
+
+    def merged(mine, theirs, axis):
+        return jnp.where(
+            first,
+            jnp.concatenate([mine, theirs], axis=axis),
+            jnp.concatenate([theirs, mine], axis=axis),
+        )
+
+    gains = jnp.stack([gain_attn, gain_mlp]).astype(F32)
+    gains = merged(gains, swap_core(gains), 1)
+    gains = jnp.concatenate([gains, swap_p(gains, 1), swap_p(gains, 2), swap_p(gains, 3)], axis=1)
+    gain_one, gain_two = gains[0:1], gains[1:2]
+    lens = jnp.concatenate([seq_lengths, swap_core(seq_lengths)], axis=0)
+
+    qkv = (query_weight.shape[1] + key_weight.shape[1] + value_weight.shape[1]) // 2
+    wide_o = output_weight.shape[0] // 2
+    keep_a, send_a, keep_o, send_o = call(
+        pack_kernel,
+        "pack",
+        (1,),
+        [(w, whole(w.shape)) for w in (query_weight, key_weight, value_weight, output_weight)],
+        [
+            ((shard, qkv), BF, whole((shard, qkv))),
+            ((shard, qkv), BF, whole((shard, qkv))),
+            ((wide_o, shard), BF, whole((wide_o, shard))),
+            ((wide_o, shard), BF, whole((wide_o, shard))),
+        ],
+        scalars=(sc,),
+    )
+    a_own = merged(keep_a, swap_core(send_a), 0)
+    a_all = jnp.stack([a_own, swap_t(a_own, 1), swap_t(a_own, 2), swap_t(a_own, 3)])
+    a_pieces = gather_p(a_all)
+    o_own = merged(keep_o, swap_core(send_o), 1)
+    o_all = jnp.stack([o_own, swap_t(o_own, 1), swap_t(o_own, 2), swap_t(o_own, 3)])
+    o_pieces = gather_p(o_all)
+
+    ff = w_gate.shape[1] // 2
+    trio = jnp.stack([w_gate, w_up, w_down.T])
+    mine = jnp.where(first, trio[:, :, :ff], trio[:, :, ff:])
+    other = jnp.where(first, trio[:, :, ff:], trio[:, :, :ff])
+    trio = merged(mine, swap_core(other), 1)
+    far_trio = swap_t(trio, 2)
+    gu_all = jnp.concatenate([trio[:2], far_trio[:2]], axis=0)
+    d_all = jnp.concatenate([trio[2:], far_trio[2:]], axis=0)
+    gu_pieces = gather_p(gu_all)
+    d_pieces = gather_p(d_all)
+
+    tile = rows // 4
+    row_full = pl.BlockSpec((tile, width), lambda i, s: (i, 0))
+    gain_spec = pl.BlockSpec((1, width), lambda i, s: (0, 0))
+    (n_one,) = call(
+        norm_one_kernel,
+        "norm_one",
+        (4,),
+        four(hidden_in, tile, quarter) + [(gain_one, gain_spec)],
+        [((rows, width), BF, row_full)],
+        scalars=(sp,),
+    )
+    (cot,) = call(
+        cast_kernel, "cot", (4,), four(cotangent, tile, quarter), [((rows, width), BF, row_full)], scalars=(sp,)
+    )
+    near = shift_up(n_one)
+    far = shift_up(near)
+    xs = (n_one, swap_core(n_one), near, swap_core(near), far, swap_core(far))
+
+    token = jnp.arange(3 * rows, dtype=jnp.int32) + level * rows - 2 * rows
+    ends = jnp.cumsum(lens, axis=1)
+    starts = jnp.sum(
+        jnp.where(token[None, :, None] >= ends[:, None, :], lens[:, None, :], 0), axis=2
+    )
+    cosine, sine = rope_tables((token[None, :] - starts).reshape(-1), HEAD_SIZE)
+    cosine = jnp.concatenate([cosine, cosine], axis=1).reshape(2, 3 * rows, HEAD_SIZE)
+    sine = jnp.concatenate([-sine, sine], axis=1).reshape(2, 3 * rows, HEAD_SIZE)
+
+    def per_j(shape, offset=0):
+        tail = (0,) * (len(shape) - 1)
+        return pl.BlockSpec((1,) + tuple(shape[1:]), lambda j, *_: (j + offset,) + tail)
+
+    def top_j(shape):
+        tail = (0,) * (len(shape) - 1)
+        return pl.BlockSpec((1,) + tuple(shape[1:]), lambda j, *_: (jnp.minimum(j, 1),) + tail)
+
+    def bottom_j(shape):
+        tail = (0,) * (len(shape) - 1)
+        return pl.BlockSpec((1,) + tuple(shape[1:]), lambda j, *_: (jnp.maximum(j - 2, 0),) + tail)
+
+    def piece_specs(pieces):
+        kinds = (per_j, per_j, per_j, top_j, bottom_j)
+        return [(x, kind(x.shape)) for x, kind in zip(pieces, kinds)]
+
+    e = HEAD_SIZE
+    q_shape, k_shape = (4, 2, 2, rows, e), (4, 2, 3 * rows, e)
+    o_shape, l_shape = (4, 2, rows, 2 * e), (4, 2, 2, rows, 1)
+    q_rot, k_rot, v_all, mixed, lse = call(
+        attention_kernel,
+        "attention",
+        (4,),
+        [(x, whole(x.shape)) for x in xs]
+        + piece_specs(a_pieces)
+        + [(cosine, whole(cosine.shape)), (sine, whole(sine.shape))],
+        [
+            (q_shape, BF, per_j(q_shape)),
+            (k_shape, BF, per_j(k_shape)),
+            (k_shape, BF, per_j(k_shape)),
+            (o_shape, BF, per_j(o_shape)),
+            (l_shape, F32, per_j(l_shape)),
+        ],
+        scalars=(sp, lens),
+        flops=12e9,
+    )
+    flat = (rows, width)
+    own, send = call(
+        project_kernel,
+        "project",
+        (1,),
+        [(mixed, whole(mixed.shape))] + [(w, whole(w.shape)) for w in o_pieces],
+        [(flat, F32, whole(flat)), (flat, BF, whole(flat))],
+        flops=1.3e9,
+    )
+    recv = swap_core(send)
+    resid, n_two = call(
+        norm_two_kernel,
+        "norm_two",
+        (4,),
+        four(hidden_in, tile, quarter) + [(own, row_full), (recv, row_full), (gain_two, gain_spec)],
+        [(flat, F32, row_full), (flat, BF, row_full)],
+        scalars=(sp,),
+    )
+
+    n_far = swap_t(n_two, 1)
+    hs = (swap_core(n_far), swap_core(n_two), n_far, n_two)
+    cot_far = swap_t(cot, 1)
+    cots = (swap_core(cot_far), swap_core(cot), cot_far, cot)
+    half = ff // 2
+
+    def unit_specs(pieces, count):
+        out = []
+        for i, x in enumerate(pieces):
+            if i < 3:
+                spec = pl.BlockSpec((count, quarter, half), lambda q, h: (q, 0, h))
+            else:
+                spec = pl.BlockSpec((count, quarter, half), lambda q, h: (0, 0, h))
+            out.append((x, spec))
+        return out
+
+    tokens = 4 * rows
+    z_shape = (3, 2, tokens, ff)
+    (z,) = call(
+        hidden_kernel,
+        "hidden",
+        (2, 2),
+        [(x, whole(x.shape)) for x in hs + cots] + unit_specs(gu_pieces, 2) + unit_specs(d_pieces, 1),
+        [(z_shape, BF, pl.BlockSpec((3, 1, tokens, half), lambda q, h: (0, q, 0, h)))],
+        flops=9.7e9,
+    )
+    two = (2, rows, width)
+    send_spec = pl.BlockSpec((1, rows, width), lambda i: (jnp.minimum(i, 1), 0, 0))
+    keep_spec = pl.BlockSpec((1, rows, width), lambda i: (jnp.maximum(i - 2, 0), 0, 0))
+
+    def hidden_back(name, at, count, pieces):
+        return call(
+            lambda *refs: hidden_back_kernel(count, *refs),
+            name,
+            (4,),
+            [(z, pl.BlockSpec((count, 2, rows, ff), lambda i: (at, 0, i, 0)))]
+            + [(w, whole(w.shape)) for w in pieces],
+            [(two, BF, send_spec), (two, BF, keep_spec)],
+            flops=count * 3.2e9,
+        )
+
+    def to_owner(send, keep):
+        recv = swap_core(send)
+        pair = (keep[0].astype(F32) + recv[0].astype(F32)).astype(BF)
+        return keep, recv, swap_t(pair, 1)
+
+    g_send, g_keep = hidden_back("hidden_back", 0, 2, gu_pieces)
+    g_keep, g_recv, g_far = to_owner(g_send, g_keep)
+
+    def second(shape):
+        return pl.BlockSpec((1, tile, width), lambda i, s: (1, i, 0))
+
+    grad_resid, low, gsum_two = call(
+        back_two_kernel,
+        "back_two",
+        (4,),
+        four(cotangent, tile, quarter)
+        + [(g_keep, second(two)), (g_recv, second(two)), (g_far, row_full), (resid, row_full), (gain_two, gain_spec)],
+        [(flat, F32, row_full), (flat, BF, row_full), ((1, width), F32, gain_spec)],
+        scalars=(sp,),
+    )
+    lows = (low, swap_core(low))
+
+    g_shape = (3, quarter, ff)
+
+    def hidden_grad(q):
+        return call(
+            hidden_grad_kernel,
+            "hidden_grad",
+            (3,),
+            [(x, whole(x.shape)) for x in hs + cots]
+            + [(z, pl.BlockSpec((1, 1, tokens, ff), lambda m: (m, q, 0, 0)))],
+            [(g_shape, BF, pl.BlockSpec((1, quarter, ff), lambda m: (m, 0, 0)))] * 4,
+            scratch=[pltpu.VMEM((width, tokens), BF)],
+            flops=4.8e9,
+        )
+
+    grads_b = hidden_grad(1)
+    grads_a = hidden_grad(0)
+    sum_a, sum_b = reduce_p(grads_a, grads_b)
+    f_far = swap_t(added(sum_b).astype(BF), 2)
+    f_total = added(sum_a) + f_far.astype(F32)
+
+    b_send, b_keep = hidden_back("hidden_out", 2, 1, d_pieces)
+    b_keep, b_recv, b_far = to_owner(b_send, b_keep)
+    (block_out,) = call(
+        block_out_kernel,
+        "block_out",
+        (4,),
+        [(resid, row_full), (b_keep, second(two)), (b_recv, second(two)), (b_far, row_full)],
+        [(flat, F32, row_full)],
+        scalars=(sp,),
+    )
+
+    og_half = (2, wide_o, quarter)
+    og = call(
+        output_grad_kernel,
+        "output_grad",
+        (1,),
+        [(x, whole(x.shape)) for x in lows + (mixed,)],
+        [(og_half, BF, whole(og_half))] * 8,
+        flops=1.3e9,
+    )
+    o_sum_a, o_sum_b = reduce_p(og[0::2], og[1::2])
+
+    d_shape, n_shape = (2, 2, rows, 4 * e), (2, 2, rows, 256)
+    ga_half = (2, quarter, qkv)
+
+    def attention_back(j0, third):
+        def at(x):
+            return (x, per_j(x.shape, j0))
+
+        return call(
+            attention_back_kernel,
+            "attention_back",
+            (2,),
+            [(x, whole(x.shape)) for x in lows]
+            + [at(x) for x in o_pieces[:3]]
+            + [(third, per_j(third.shape))]
+            + [at(x) for x in (q_rot, k_rot, v_all, mixed, lse)]
+            + [(cosine, whole(cosine.shape)), (sine, whole(sine.shape))],
+            [
+                (d_shape, BF, per_j(d_shape)),
+                (n_shape, BF, per_j(n_shape)),
+                (n_shape, BF, per_j(n_shape)),
+            ],
+            scalars=(sp, lens),
+            flops=4e9,
+        )
+
+    def attention_grad(ds):
+        return call(
+            attention_grad_kernel,
+            "attention_grad",
+            (2,),
+            [(x, whole(x.shape)) for x in xs] + [(d, per_j(d.shape)) for d in ds],
+            [(ga_half, BF, per_j(ga_half))] * 4,
+            scratch=[pltpu.VMEM((width, 6 * rows), BF)],
+            flops=5e9,
+        )
+
+    ds_b = attention_back(2, o_pieces[4])
+    ag_b = attention_grad(ds_b)
+    ds_a = attention_back(0, o_pieces[3])
+    ag_a = attention_grad(ds_a)
+    a_sum_a, a_sum_b = reduce_p(ag_a, ag_b)
+
+    d_own, d_near, d_far = (jnp.concatenate([a, b], axis=0) for a, b in zip(ds_a, ds_b))
+    even = level % 2 == 0
+
+    def refit(x):
+        pairs = jnp.concatenate([x[1:2], x[0:1], x[3:4], x[2:3]], axis=0)
+        back = jnp.concatenate([x[3:4], x[2:3], x[1:2], x[0:1]], axis=0)
+        return jnp.where(even, pairs, back)
+
+    s_near = (d_near.astype(F32) + refit(shift_down(d_far)).astype(F32)).astype(BF)
+    s_near = refit(shift_down(s_near))
+    own, send = call(
+        inner_back_kernel,
+        "inner_back",
+        (1,),
+        [(x, whole(x.shape)) for x in (d_own, s_near) + tuple(a_pieces)],
+        [(flat, F32, whole(flat)), (flat, BF, whole(flat))],
+        flops=2.5e9,
+    )
+    recv = swap_core(send)
+    grad_input, gsum_one = call(
+        back_one_kernel,
+        "back_one",
+        (4,),
+        four(hidden_in, tile, quarter)
+        + [(own, row_full), (recv, row_full), (grad_resid, row_full), (gain_one, gain_spec)],
+        [(flat, F32, row_full), ((1, width), F32, gain_spec)],
+        scalars=(sp,),
+    )
+
+    def over_levels(sum_a, sum_b):
+        to = [added(sum_a, 1), added(sum_b, 0), added(sum_b, 1)]
+        total = added(sum_a, 0)
+        for k in range(3):
+            total = total + swap_t(to[k].astype(BF), k + 1).astype(F32)
+        return total
+
+    a_total = over_levels(a_sum_a, a_sum_b)
+    o_total = over_levels(o_sum_a, o_sum_b)
+
+    def split(total, axis):
+        n = total.shape[axis] // 2
+        low_part = lax.slice_in_dim(total, 0, n, axis=axis)
+        high_part = lax.slice_in_dim(total, n, 2 * n, axis=axis)
+        mine = jnp.where(first, low_part, high_part)
+        theirs = swap_core(jnp.where(first, high_part, low_part).astype(BF)).astype(F32)
+        return mine, theirs
+
+    mine, theirs = split(a_total, 0)
+    cuts = (0, 2 * e, 3 * e, 4 * e)
+    grad_query, grad_key, grad_value = (
+        merged(mine[:, i:k], theirs[:, i:k], 1) for i, k in zip(cuts[:-1], cuts[1:])
+    )
+    mine, theirs = split(o_total, 1)
+    grad_output = merged(mine, theirs, 0)
+    mine, theirs = split(f_total, 1)
+    f_grads = merged(mine, theirs, 2)
+
+    gsums = jnp.concatenate([gsum_one, gsum_two], axis=0)
+    gsums = gsums + swap_core(gsums)
+    gsums = gsums + swap_t(gsums, 1)
+    gsums = gsums + swap_t(gsums, 2)
+    total = gsums[:, :quarter]
+    for k in range(1, 4):
+        total = total + swap_p(gsums[:, k * quarter : (k + 1) * quarter], k)
+    total = jnp.where(first, total[:, :shard], total[:, shard:])
+    return (
+        block_out,
+        grad_input,
+        grad_query,
+        grad_key,
+        grad_value,
+        grad_output,
+        f_grads[0],
+        f_grads[1],
+        f_grads[2].T,
+        total[0],
+        total[1],
+    )
+
+
 def solution(mesh):
+    wide = mesh.shape["dp"] == 8 and mesh.shape["tensor"] == 4
+    body = local_fast if wide else local_plain
     in_specs = (
         P(("dp", "tensor"), None),
         P(("dp", "tensor"), None),
@@ -404,4 +1183,4 @@
         P("dp"),
         P("dp"),
     )
-    return jax.shard_map(local, mesh=mesh, in_specs=in_specs, out_specs=out_specs, check_vma=False)
+    return jax.shard_map(body, mesh=mesh, in_specs=in_specs, out_specs=out_specs, check_vma=False)

time: 1100 us -> 585 us (0.53)
  waiting for transfers between devices: 749 us -> 205 us
  Pallas kernels: 0 us -> 181 us
  matrix products: 152 us -> 0 us
  starting transfers between devices: 1.92 us -> 122 us
  blocking collectives: 63.4 us -> 0 us
  local copies, waits for them, and re-layouts: 60.7 us -> 24.1 us
  between operations: 16.5 us -> 1.77 us
    reduce_scatter x11 -> x0, waiting for transfers between devices: 440 us -> none  [the longest x1 110 us: local(): lax.psum_scatter(matrix_multiply(mixed_flat, output_full), 'tensor', scat...]
    all_gather x9 -> x0, waiting for transfers between devices: 306 us -> none  [the longest x1 65.5 us: local(): normed_two = lax.all_gather(normed_rows_two, 'tensor', axis=0, tiled=True)]
    ppermute x0 -> x85, waiting for transfers between devices: none -> 205 us  [the longest x40 131 us: swap_p(): return lax.ppermute(x, 'dp', [(i, i ^ 2 * k) for i in range(8)])]
    pallas_call x0 -> x20, Pallas kernels: none -> 181 us  [call(): pl.pallas_call(kernel, name=name, out_shape=[jax.ShapeDtypeStruct(s, d) f...]
    dot_general x35 -> x0, matrix products: 152 us -> none  [the longest x14 43.7 us: product(): jnp.einsum(formula, left_side, right_side, preferred_element_type=jnp.flo...]
    ppermute x0 -> x85, starting transfers between devices: none -> 122 us  [the longest x20 65.7 us: swap_t(): return lax.ppermute(x, 'tensor', [(i, i ^ k) for i in range(4)])]
    dynamic_update_slice x4 -> x0, local copies, waits for them, and re-layouts: 31.7 us -> none  [attend_back(): lax.scan(per_block, (empty_grad, empty_grad), (queries.reshape(shape_bloc...]
    unnamed x2 -> x0, blocking collectives: 29.6 us -> none
  transfers between devices with their start and end apart: 20 -> 85, of which waited for: 17 -> 33; matrix products, arithmetic and copies ran while one was open for 20% -> 10% of each run, Pallas kernels for 0% -> 25%
where the time goes in v1:
time: 585 us; the launch traced here: 580 us
  waiting for transfers between devices  205 us (35%)
  Pallas kernels  181 us (31%)
  starting transfers between devices  122 us (21%)
  other arithmetic  46.2 us (8%)
  local copies, waits for them, and re-layouts  24.1 us (4%)
    pallas_call x20, Pallas kernels, call(): pl.pallas_call(kernel, name=name, out_shape=[jax.ShapeDtypeStruct(s, d) f...  181 us
    ppermute x40, waiting for transfers between devices, swap_p(): return lax.ppermute(x, 'dp', [(i, i ^ 2 * k) for i in range(8)])  131 us
    ppermute x20, starting transfers between devices, swap_t(): return lax.ppermute(x, 'tensor', [(i, i ^ k) for i in range(4)])  65.7 us
    ppermute x20, waiting for transfers between devices, swap_t(): return lax.ppermute(x, 'tensor', [(i, i ^ k) for i in range(4)])  59.2 us
    ppermute x40, starting transfers between devices, swap_p(): return lax.ppermute(x, 'dp', [(i, i ^ 2 * k) for i in range(8)])  39.5 us
    ppermute x2, waiting for transfers between devices, shift_up(): return lax.ppermute(x, 'tensor', [(i, i + 1) for i in range(3)])  13.5 us
  transfers between devices with their start and end apart: 85, of which 33 were waited for; matrix products, arithmetic and copies ran while one was open for 10% of the time, Pallas kernels for 25%

profile of v1, /device:TPU:0, one launch (start us, length us, event | category | flops | bytes accessed | tf_op | source)
XLA Modules:
  0.0 580.2 jit_solution(15541442021435386499)
XLA Ops:
  31.5 18.0 %collective-permute-done.12 = bf16[384,384]{1,0:T(8,128)(2,1)S(1)} collective-permute-done((bf16[384,384]{1,0:T(8,128)(2,1)S(1)}, bf16[384,384]{1,0:T(8,128)(2,1)S(1)}, u32[]{:S(2)}, u32[]{:S(2)}) %collective-permute-start.12) | collective-permute-done | bytes 294944 | tf_op jit(solution)/shard_map/ppermute | solution.py:434
  50.8 9.1 %collective-permute-done.21 = bf16[192,384]{1,0:T(8,128)(2,1)S(1)} collective-permute-done((bf16[192,384]{1,0:T(8,128)(2,1)S(1)}, bf16[192,384]{1,0:T(8,128)(2,1)S(1)}, u32[]{:S(2)}, u32[]{:S(2)}) %collective-permute-start.21) | collective-permute-done | bytes 147488 | tf_op jit(solution)/shard_map/ppermute | solution.py:434
  68.2 9.9 %collective-permute-start.34 = (bf16[3,384,512]{2,1,0:T(8,128)(2,1)S(1)}, bf16[3,384,512]{2,1,0:T(8,128)(2,1)S(1)}, u32[]{:S(2)}, u32[]{:S(2)}) collective-permute-start(bf16[3,384,512]{2,1,0:T(8,128)(2,1)S(1)} %maximum_select_fusion.1), channel_id=1, source_target_pairs={{0,2},{1,3},{2,0},{3,1},{4,6},{5,7},{6,4},{7,5},{8,10},{9,11},{10,... | collective-permute-start | bytes 3538952 | tf_op jit(solution)/shard_map/ppermute | solution.py:434
  84.4 16.7 %collective-permute-done.23.w2 = bf16[4,192,384]{2,1,0:T(8,128)(2,1)S(1)} collective-permute-done((bf16[4,192,384]{2,1,0:T(8,128)(2,1)}, bf16[4,192,384]{2,1,0:T(8,128)(2,1)S(1)}, u32[]{:S(2)}, u32[]{:S(2)}) %collective-permute-start.23) | collective-permute-done | bytes 589856 | tf_op jit(solution)/shard_map/ppermute | solution.py:430
  106.6 13.5 %collective-permute-done.8.x2 = bf16[256,1536]{1,0:T(8,128)(2,1)} collective-permute-done((bf16[256,1536]{1,0:T(8,128)(2,1)}, bf16[256,1536]{1,0:T(8,128)(2,1)}, u32[]{:S(2)}, u32[]{:S(2)}) %collective-permute-start.8) | collective-permute-done | bytes 786464 | tf_op jit(solution)/shard_map/ppermute | solution.py:438
  140.7 20.6 %collective-permute-start.30 = (bf16[256,1536]{1,0:T(8,128)(2,1)S(1)}, bf16[256,1536]{1,0:T(8,128)(2,1)}, u32[]{:S(2)}, u32[]{:S(2)}) collective-permute-start(bf16[256,1536]{1,0:T(8,128)(2,1)S(1)} %copy-done.8), channel_id=1, source_target_pairs={{0,1},{1,0},{2,3},{3,2},{4,5},{5,4},{6,7},{7,6},{8,9},{9,8},{10,11... | collective-permute-start | bytes 2359304 | tf_op jit(solution)/shard_map/ppermute | solution.py:434
  166.3 26.5 %attention.1 = (bf16[4,2,2,256,96]{4,3,2,1,0:T(8,128)(2,1)}, bf16[4,2,768,96]{3,2,1,0:T(8,128)(2,1)}, bf16[4,2,768,96]{3,2,1,0:T(8,128)(2,1)}, bf16[4,2,256,192]{3,2,1,0:T(8,128)(2,1)}, f32[4,2,2,256,1]{4,3,2,1,0:T(8,128)}) custom-call(s32[3]{0:T(128)} %pad_add_fusion.1.s, s32[2,4]{1,0:T(2,128)} %copy-done.32, bf16[256,1536]{1,0:T(8,128)(2,1)} %norm_one.1.x0, ...), custom_call_target="tpu_custom_call" | custom-call | flops 12000000000 | bytes 14565376 | tf_op jit(solution)/shard_map/attention/pallas_call | solution.py:407
  206.9 15.1 %collective-permute-done.40.d2.refs_3_ = bf16[2,384,512]{2,1,0:T(8,128)(2,1)S(1)} collective-permute-done((bf16[2,384,512]{2,1,0:T(8,128)(2,1)}, bf16[2,384,512]{2,1,0:T(8,128)(2,1)S(1)}, u32[]{:S(2)}, u32[]{:S(2)}) %collective-permute-start.40) | collective-permute-done | bytes 786464 | tf_op jit(solution)/shard_map/ppermute | solution.py:430
  229.4 13.3 %collective-permute-done.39.d1.refs_2_ = bf16[2,384,512]{2,1,0:T(8,128)(2,1)S(1)} collective-permute-done((bf16[2,384,512]{2,1,0:T(8,128)(2,1)}, bf16[2,384,512]{2,1,0:T(8,128)(2,1)S(1)}, u32[]{:S(2)}, u32[]{:S(2)}) %collective-permute-start.39) | collective-permute-done | bytes 786464 | tf_op jit(solution)/shard_map/ppermute | solution.py:430
  243.2 7.9 %collective-permute-done.42.d3b.refs_5_ = bf16[1,384,512]{2,1,0:T(8,128)(2,1)S(1)} collective-permute-done((bf16[1,384,512]{2,1,0:T(8,128)(2,1)S(1)}, bf16[1,384,512]{2,1,0:T(8,128)(2,1)S(1)}, u32[]{:S(2)}, u32[]{:S(2)}) %collective-permute-start.42) | collective-permute-done | bytes 393248 | tf_op jit(solution)/shard_map/ppermute | solution.py:430
  251.5 14.1 %collective-permute-done.41.d3t.refs_4_ = bf16[1,384,512]{2,1,0:T(8,128)(2,1)S(1)} collective-permute-done((bf16[1,384,512]{2,1,0:T(8,128)(2,1)S(1)}, bf16[1,384,512]{2,1,0:T(8,128)(2,1)S(1)}, u32[]{:S(2)}, u32[]{:S(2)}) %collective-permute-start.41) | collective-permute-done | bytes 393248 | tf_op jit(solution)/shard_map/ppermute | solution.py:430
  268.2 16.1 %hidden.1.refs_0_.z = bf16[3,2,1024,512]{3,2,1,0:T(8,128)(2,1)} custom-call(bf16[256,1536]{1,0:T(8,128)(2,1)} %copy-done.40, bf16[256,1536]{1,0:T(8,128)(2,1)} %copy-done.39, bf16[256,1536]{1,0:T(8,128)(2,1)} %copy-done.38, bf16[256,1536]{1,0:T(8,128)(2,1)} %get-tuple-element.73.x3, bf16[256,1536]{1,0:T(8,128)(2,1)} %collective-permute-done.31.c0, ...), custom_call_target="tpu_custom_call" | custom-call | flops 9699999744 | bytes 22020096 | tf_op jit(solution)/shard_map/hidden/pallas_call | solution.py:407
  284.2 14.1 %hidden_back.1 = (bf16[2,256,1536]{2,1,0:T(8,128)(2,1)}, bf16[2,256,1536]{2,1,0:T(8,128)(2,1)}) custom-call(bf16[3,2,1024,512]{3,2,1,0:T(8,128)(2,1)} %hidden.1.refs_0_.z, bf16[4,384,512]{2,1,0:T(8,128)(2,1)} %copy-done.4, bf16[4,384,512]{2,1,0:T(8,128)(2,1)} %collective-permute-done.35.a1.refs_2_, bf16[4,384,512]{2,1,0:T(8,128)(2,1)} %collective-permute-done.36.a2.refs_3_, ...), custom_call_target="tpu_custom_call" | custom-call | flops 6400000000 | bytes 15728640 | tf_op jit(solution)/shard_map/hidden_back/pallas_call | solution.py:407
  298.4 8.7 %hidden_out.1 = (bf16[2,256,1536]{2,1,0:T(8,128)(2,1)}, bf16[2,256,1536]{2,1,0:T(8,128)(2,1)}) custom-call(bf16[3,2,1024,512]{3,2,1,0:T(8,128)(2,1)} %hidden.1.refs_0_.z, bf16[2,384,512]{2,1,0:T(8,128)(2,1)} %pad_maximum_fusion.7.d0.refs_1_, bf16[2,384,512]{2,1,0:T(8,128)(2,1)} %copy-done.28, bf16[2,384,512]{2,1,0:T(8,128)(2,1)} %copy-done.27, ...), custom_call_target="tpu_custom_call" | custom-call | flops 3200000000 | bytes 12582912 | tf_op jit(solution)/shard_map/hidden_out/pallas_call | solution.py:407
  307.5 11.4 %hidden_grad.3 = (bf16[3,384,512]{2,1,0:T(8,128)(2,1)}, bf16[3,384,512]{2,1,0:T(8,128)(2,1)}, bf16[3,384,512]{2,1,0:T(8,128)(2,1)}, bf16[3,384,512]{2,1,0:T(8,128)(2,1)}) custom-call(bf16[256,1536]{1,0:T(8,128)(2,1)} %copy-done.40, bf16[256,1536]{1,0:T(8,128)(2,1)} %copy-done.39, bf16[256,1536]{1,0:T(8,128)(2,1)} %copy-done.38, ...), custom_call_target="tpu_custom_call" | custom-call | flops 4800000000 | bytes 17301504 | tf_op jit(solution)/shard_map/hidden_grad/pallas_call | solution.py:407
  326.6 11.6 %hidden_grad.2 = (bf16[3,384,512]{2,1,0:T(8,128)(2,1)}, bf16[3,384,512]{2,1,0:T(8,128)(2,1)}, bf16[3,384,512]{2,1,0:T(8,128)(2,1)}, bf16[3,384,512]{2,1,0:T(8,128)(2,1)}) custom-call(bf16[256,1536]{1,0:T(8,128)(2,1)} %copy-done.40, bf16[256,1536]{1,0:T(8,128)(2,1)} %copy-done.39, bf16[256,1536]{1,0:T(8,128)(2,1)} %copy-done.38, ...), custom_call_target="tpu_custom_call" | custom-call | flops 4800000000 | bytes 17301504 | tf_op jit(solution)/shard_map/hidden_grad/pallas_call | solution.py:407
  339.1 9.0 %collective-permute-done.75 = bf16[3,384,512]{2,1,0:T(8,128)(2,1)} collective-permute-done((bf16[3,384,512]{2,1,0:T(8,128)(2,1)}, bf16[3,384,512]{2,1,0:T(8,128)(2,1)}, u32[]{:S(2)}, u32[]{:S(2)}) %collective-permute-start.75) | collective-permute-done | bytes 1179680 | tf_op jit(solution)/shard_map/ppermute | solution.py:430
  374.4 18.3 %collective-permute-done.76 = bf16[3,384,512]{2,1,0:T(8,128)(2,1)} collective-permute-done((bf16[3,384,512]{2,1,0:T(8,128)(2,1)}, bf16[3,384,512]{2,1,0:T(8,128)(2,1)}, u32[]{:S(2)}, u32[]{:S(2)}) %collective-permute-start.76) | collective-permute-done | bytes 1179680 | tf_op jit(solution)/shard_map/ppermute | solution.py:430
  407.7 13.2 %attention_back.2 = (bf16[2,2,256,384]{3,2,1,0:T(8,128)(2,1)}, bf16[2,2,256,256]{3,2,1,0:T(8,128)(2,1)}, bf16[2,2,256,256]{3,2,1,0:T(8,128)(2,1)}) custom-call(s32[3]{0:T(128)} %pad_add_fusion.1.s, s32[2,4]{1,0:T(2,128)} %copy-done.32, bf16[256,1536]{1,0:T(8,128)(2,1)} %get-tuple-element.78.n0, bf16[256,1536]{1,0:T(8,128)(2,1)} %collective-permute-done.47.n1, ...), custom_call_target="tpu_custom_call" | custom-call | flops 4000000000 | bytes 10600448 | tf_op jit(solution)/shard_map/attention_back/pallas_call | solution.py:407
  420.9 8.8 %attention_grad.2 = (bf16[2,384,384]{2,1,0:T(8,128)(2,1)}, bf16[2,384,384]{2,1,0:T(8,128)(2,1)}, bf16[2,384,384]{2,1,0:T(8,128)(2,1)}, bf16[2,384,384]{2,1,0:T(8,128)(2,1)}) custom-call(bf16[256,1536]{1,0:T(8,128)(2,1)} %norm_one.1.x0, bf16[256,1536]{1,0:T(8,128)(2,1)} %copy-done.34, bf16[256,1536]{1,0:T(8,128)(2,1)} %collective-permute-done.6.x1, ...), custom_call_target="tpu_custom_call" | custom-call | flops 5000000000 | bytes 8912896 | tf_op jit(solution)/shard_map/attention_grad/pallas_call | solution.py:407
  429.7 13.3 %attention_back.3 = (bf16[2,2,256,384]{3,2,1,0:T(8,128)(2,1)}, bf16[2,2,256,256]{3,2,1,0:T(8,128)(2,1)}, bf16[2,2,256,256]{3,2,1,0:T(8,128)(2,1)}) custom-call(s32[3]{0:T(128)} %pad_add_fusion.1.s, s32[2,4]{1,0:T(2,128)} %copy-done.32, bf16[256,1536]{1,0:T(8,128)(2,1)} %get-tuple-element.78.n0, bf16[256,1536]{1,0:T(8,128)(2,1)} %collective-permute-done.47.n1, ...), custom_call_target="tpu_custom_call" | custom-call | flops 4000000000 | bytes 10600448 | tf_op jit(solution)/shard_map/attention_back/pallas_call | solution.py:407
  443.0 8.4 %attention_grad.3 = (bf16[2,384,384]{2,1,0:T(8,128)(2,1)}, bf16[2,384,384]{2,1,0:T(8,128)(2,1)}, bf16[2,384,384]{2,1,0:T(8,128)(2,1)}, bf16[2,384,384]{2,1,0:T(8,128)(2,1)}) custom-call(bf16[256,1536]{1,0:T(8,128)(2,1)} %norm_one.1.x0, bf16[256,1536]{1,0:T(8,128)(2,1)} %copy-done.34, bf16[256,1536]{1,0:T(8,128)(2,1)} %collective-permute-done.6.x1, ...), custom_call_target="tpu_custom_call" | custom-call | flops 5000000000 | bytes 8912896 | tf_op jit(solution)/shard_map/attention_grad/pallas_call | solution.py:407
  531.5 7.9 %inner_back.1 = (f32[256,1536]{1,0:T(8,128)}, bf16[256,1536]{1,0:T(8,128)(2,1)}) custom-call(bf16[4,2,256,384]{3,2,1,0:T(8,128)(2,1)} %pad_maximum_fusion.1.d_own, bf16[4,2,256,256]{3,2,1,0:T(8,128)(2,1)} %maximum_select_fusion.3.s_near, bf16[4,384,384]{2,1,0:T(8,128)(2,1)} %pad_maximum_fusion.2.w0, bf16[4,384,384]{2,1,0:T(8,128)(2,1)} %collective-permute-done.14.w1, ...), custom_call_target="tpu_custom_call" | custom-call | flops 2500000000 | bytes 9699328 | tf_op jit(solution)/shard_map/inner_back/pallas_call | solution.py:407
  541.0 8.4 %collective-permute-done.58 = bf16[384,384]{1,0:T(8,128)(2,1)} collective-permute-done((bf16[384,384]{1,0:T(8,128)(2,1)}, bf16[384,384]{1,0:T(8,128)(2,1)}, u32[]{:S(2)}, u32[]{:S(2)}) %collective-permute-start.58) | collective-permute-done | bytes 294944 | tf_op jit(solution)/shard_map/ppermute | solution.py:434
  (362 shorter events, 264.6 us)
Async XLA Ops:
  13.4 52.7 %collective-permute-start.33 = (bf16[3,192,512]{2,1,0:T(8,128)(2,1)S(1)}, bf16[3,192,512]{2,1,0:T(8,128)(2,1)S(1)}, u32[]{:S(2)}, u32[]{:S(2)}) collective-permute-start(bf16[3,192,512]{2,1,0:T(8,128)(2,1)S(1)} %get-tuple-element.147), channel_id=1, source_target_pairs={{0,4},{4,0},{8,12},{12,8},{16,20},{20,16},{24,28},{28,24},{1,5},{5... | collective-permute-start | bytes 1769480 | tf_op jit(solution)/shard_map/ppermute | solution.py:426
  25.7 52.4 %collective-permute-start.6 = (bf16[256,1536]{1,0:T(8,128)(2,1)}, bf16[256,1536]{1,0:T(8,128)(2,1)}, u32[]{:S(2)}, u32[]{:S(2)}) collective-permute-start(bf16[256,1536]{1,0:T(8,128)(2,1)} %norm_one.1.x0), channel_id=1, source_target_pairs={{0,1},{1,2},{2,3},{4,5},{5,6},{6,7},{8,9},{9,10},{10,11},{12,13},{... | collective-permute-start | bytes 2359304 | tf_op jit(solution)/shard_map/ppermute | solution.py:438
  62.5 57.6 %collective-permute-start.15 = (bf16[4,384,384]{2,1,0:T(8,128)(2,1)}, bf16[4,384,384]{2,1,0:T(8,128)(2,1)}, u32[]{:S(2)}, u32[]{:S(2)}) collective-permute-start(bf16[4,384,384]{2,1,0:T(8,128)(2,1)} %pad_maximum_fusion.2.w0), channel_id=1, source_target_pairs={{0,16},{4,20},{8,24},{12,28},{16,0},{20,4},{24,8},{28,12},{1,17},{... | collective-permute-start | bytes 3538952 | tf_op jit(solution)/shard_map/ppermute | solution.py:430
  64.0 56.6 %collective-permute-start.14 = (bf16[4,384,384]{2,1,0:T(8,128)(2,1)}, bf16[4,384,384]{2,1,0:T(8,128)(2,1)}, u32[]{:S(2)}, u32[]{:S(2)}) collective-permute-start(bf16[4,384,384]{2,1,0:T(8,128)(2,1)} %pad_maximum_fusion.2.w0), channel_id=1, source_target_pairs={{0,8},{4,12},{8,0},{12,4},{16,24},{20,28},{24,16},{28,20},{1,9},{5... | collective-permute-start | bytes 3538952 | tf_op jit(solution)/shard_map/ppermute | solution.py:430
  68.2 60.9 %collective-permute-start.34 = (bf16[3,384,512]{2,1,0:T(8,128)(2,1)S(1)}, bf16[3,384,512]{2,1,0:T(8,128)(2,1)S(1)}, u32[]{:S(2)}, u32[]{:S(2)}) collective-permute-start(bf16[3,384,512]{2,1,0:T(8,128)(2,1)S(1)} %maximum_select_fusion.1), channel_id=1, source_target_pairs={{0,2},{1,3},{2,0},{3,1},{4,6},{5,7},{6,4},{7,5},{8,10},{9,11},{10,... | collective-permute-start | bytes 3538952 | tf_op jit(solution)/shard_map/ppermute | solution.py:434
  78.1 42.0 %collective-permute-start.8 = (bf16[256,1536]{1,0:T(8,128)(2,1)}, bf16[256,1536]{1,0:T(8,128)(2,1)}, u32[]{:S(2)}, u32[]{:S(2)}) collective-permute-start(bf16[256,1536]{1,0:T(8,128)(2,1)} %collective-permute-done.6.x1), channel_id=1, source_target_pairs={{0,1},{1,2},{2,3},{4,5},{5,6},{6,7},{8,9},{9,10},{10,11},{12,13},{... | collective-permute-start | bytes 2359304 | tf_op jit(solution)/shard_map/ppermute | solution.py:438
  120.1 41.2 %collective-permute-start.7 = (bf16[256,1536]{1,0:T(8,128)(2,1)}, bf16[256,1536]{1,0:T(8,128)(2,1)S(1)}, u32[]{:S(2)}, u32[]{:S(2)}) collective-permute-start(bf16[256,1536]{1,0:T(8,128)(2,1)} %collective-permute-done.6.x1), channel_id=1, source_target_pairs={{0,4},{4,0},{8,12},{12,8},{16,20},{20,16},{24,28},{28,24},{1,5},{5... | collective-permute-start | bytes 2359304 | tf_op jit(solution)/shard_map/ppermute | solution.py:426
  120.6 44.5 %collective-permute-start.9 = (bf16[256,1536]{1,0:T(8,128)(2,1)}, bf16[256,1536]{1,0:T(8,128)(2,1)S(1)}, u32[]{:S(2)}, u32[]{:S(2)}) collective-permute-start(bf16[256,1536]{1,0:T(8,128)(2,1)} %collective-permute-done.8.x2), channel_id=1, source_target_pairs={{0,4},{4,0},{8,12},{12,8},{16,20},{20,16},{24,28},{28,24},{1,5},{5... | collective-permute-start | bytes 2359304 | tf_op jit(solution)/shard_map/ppermute | solution.py:426
  123.0 40.1 %collective-permute-start.17 = (bf16[2,384,384]{2,1,0:T(8,128)(2,1)S(1)}, bf16[2,384,384]{2,1,0:T(8,128)(2,1)S(1)}, u32[]{:S(2)}, u32[]{:S(2)}) collective-permute-start(bf16[2,384,384]{2,1,0:T(8,128)(2,1)S(1)} %slice.312), channel_id=1, source_target_pairs={{0,8},{4,12},{8,0},{12,4},{16,24},{20,28},{24,16},{28,20},{1,9},{5... | collective-permute-start | bytes 1769480 | tf_op jit(solution)/shard_map/ppermute | solution.py:430
  140.7 59.7 %collective-permute-start.30 = (bf16[256,1536]{1,0:T(8,128)(2,1)S(1)}, bf16[256,1536]{1,0:T(8,128)(2,1)}, u32[]{:S(2)}, u32[]{:S(2)}) collective-permute-start(bf16[256,1536]{1,0:T(8,128)(2,1)S(1)} %copy-done.8), channel_id=1, source_target_pairs={{0,1},{1,0},{2,3},{3,2},{4,5},{5,4},{6,7},{7,6},{8,9},{9,8},{10,11... | collective-permute-start | bytes 2359304 | tf_op jit(solution)/shard_map/ppermute | solution.py:434
  163.5 58.9 %collective-permute-start.36 = (bf16[4,384,512]{2,1,0:T(8,128)(2,1)S(1)}, bf16[4,384,512]{2,1,0:T(8,128)(2,1)}, u32[]{:S(2)}, u32[]{:S(2)}) collective-permute-start(bf16[4,384,512]{2,1,0:T(8,128)(2,1)S(1)} %pad_maximum_fusion.a0.refs_1_), channel_id=1, source_target_pairs={{0,16},{4,20},{8,24},{12,28},{16,0},{20,4},{24,8},{28,12},{1,17},{... | collective-permute-start | bytes 4718600 | tf_op jit(solution)/shard_map/ppermute | solution.py:430
  166.0 59.9 %collective-permute-start.35 = (bf16[4,384,512]{2,1,0:T(8,128)(2,1)S(1)}, bf16[4,384,512]{2,1,0:T(8,128)(2,1)}, u32[]{:S(2)}, u32[]{:S(2)}) collective-permute-start(bf16[4,384,512]{2,1,0:T(8,128)(2,1)S(1)} %pad_maximum_fusion.a0.refs_1_), channel_id=1, source_target_pairs={{0,8},{4,12},{8,0},{12,4},{16,24},{20,28},{24,16},{28,20},{1,9},{5... | collective-permute-start | bytes 4718600 | tf_op jit(solution)/shard_map/ppermute | solution.py:430
  228.9 36.7 %collective-permute-start.29 = (bf16[256,1536]{1,0:T(8,128)(2,1)S(1)}, bf16[256,1536]{1,0:T(8,128)(2,1)S(1)}, u32[]{:S(2)}, u32[]{:S(2)}) collective-permute-start(bf16[256,1536]{1,0:T(8,128)(2,1)S(1)} %copy-done.37), channel_id=1, source_target_pairs={{0,4},{4,0},{8,12},{12,8},{16,20},{20,16},{24,28},{28,24},{1,5},{5... | collective-permute-start | bytes 2359304 | tf_op jit(solution)/shard_map/ppermute | solution.py:426
  229.0 36.6 %collective-permute-start.38 = (bf16[2,384,512]{2,1,0:T(8,128)(2,1)S(1)}, bf16[2,384,512]{2,1,0:T(8,128)(2,1)S(1)}, u32[]{:S(2)}, u32[]{:S(2)}) collective-permute-start(bf16[2,384,512]{2,1,0:T(8,128)(2,1)S(1)} %slice.321), channel_id=1, source_target_pairs={{0,8},{4,12},{8,0},{12,4},{16,24},{20,28},{24,16},{28,20},{1,9},{5... | collective-permute-start | bytes 2359304 | tf_op jit(solution)/shard_map/ppermute | solution.py:430
  307.1 45.1 %collective-permute-start.43 = (bf16[2,256,1536]{2,1,0:T(8,128)(2,1)}, bf16[2,256,1536]{2,1,0:T(8,128)(2,1)S(1)}, u32[]{:S(2)}, u32[]{:S(2)}) collective-permute-start(bf16[2,256,1536]{2,1,0:T(8,128)(2,1)} %get-tuple-element.75), channel_id=1, source_target_pairs={{0,4},{4,0},{8,12},{12,8},{16,20},{20,16},{24,28},{28,24},{1,5},{5... | collective-permute-start | bytes 4718600 | tf_op jit(solution)/shard_map/ppermute | solution.py:426
  351.2 41.4 %collective-permute-start.76 = (bf16[3,384,512]{2,1,0:T(8,128)(2,1)}, bf16[3,384,512]{2,1,0:T(8,128)(2,1)}, u32[]{:S(2)}, u32[]{:S(2)}) collective-permute-start(bf16[3,384,512]{2,1,0:T(8,128)(2,1)} %add.218), channel_id=1, source_target_pairs={{0,16},{4,20},{8,24},{12,28},{16,0},{20,4},{24,8},{28,12},{1,17},{... | collective-permute-start | bytes 3538952 | tf_op jit(solution)/shard_map/ppermute | solution.py:430
  353.4 44.4 %collective-permute-start.44 = (bf16[256,1536]{1,0:T(8,128)(2,1)}, bf16[256,1536]{1,0:T(8,128)(2,1)}, u32[]{:S(2)}, u32[]{:S(2)}) collective-permute-start(bf16[256,1536]{1,0:T(8,128)(2,1)} %fusion), channel_id=1, source_target_pairs={{0,1},{1,0},{2,3},{3,2},{4,5},{5,4},{6,7},{7,6},{8,9},{9,8},{10,11... | collective-permute-start | bytes 2359304 | tf_op jit(solution)/shard_map/ppermute | solution.py:434
  362.5 40.0 %collective-permute-start.47 = (bf16[256,1536]{1,0:T(8,128)(2,1)}, bf16[256,1536]{1,0:T(8,128)(2,1)}, u32[]{:S(2)}, u32[]{:S(2)}) collective-permute-start(bf16[256,1536]{1,0:T(8,128)(2,1)} %get-tuple-element.78.n0), channel_id=1, source_target_pairs={{0,4},{4,0},{8,12},{12,8},{16,20},{20,16},{24,28},{28,24},{1,5},{5... | collective-permute-start | bytes 2359304 | tf_op jit(solution)/shard_map/ppermute | solution.py:426
  367.4 92.3 %collective-permute-start.73 = (bf16[3,384,512]{2,1,0:T(8,128)(2,1)}, bf16[3,384,512]{2,1,0:T(8,128)(2,1)S(1)}, u32[]{:S(2)}, u32[]{:S(2)}) collective-permute-start(bf16[3,384,512]{2,1,0:T(8,128)(2,1)} %get-tuple-element.112), channel_id=1, source_target_pairs={{0,16},{4,20},{8,24},{12,28},{16,0},{20,4},{24,8},{28,12},{1,17},{... | collective-permute-start | bytes 3538952 | tf_op jit(solution)/shard_map/ppermute | solution.py:430
  372.6 88.5 %collective-permute-start.72 = (bf16[3,384,512]{2,1,0:T(8,128)(2,1)S(1)}, bf16[3,384,512]{2,1,0:T(8,128)(2,1)S(1)}, u32[]{:S(2)}, u32[]{:S(2)}) collective-permute-start(bf16[3,384,512]{2,1,0:T(8,128)(2,1)S(1)} %add.214), channel_id=1, source_target_pairs={{0,8},{4,12},{8,0},{12,4},{16,24},{20,28},{24,16},{28,20},{1,9},{5... | collective-permute-start | bytes 3538952 | tf_op jit(solution)/shard_map/ppermute | solution.py:430
  395.8 65.5 %collective-permute-start.77 = (bf16[3,384,512]{2,1,0:T(8,128)(2,1)}, bf16[3,384,512]{2,1,0:T(8,128)(2,1)}, u32[]{:S(2)}, u32[]{:S(2)}) collective-permute-start(bf16[3,384,512]{2,1,0:T(8,128)(2,1)} %add_convert_fusion), channel_id=1, source_target_pairs={{0,2},{1,3},{2,0},{3,1},{4,6},{5,7},{6,4},{7,5},{8,10},{9,11},{10,... | collective-permute-start | bytes 3538952 | tf_op jit(solution)/shard_map/ppermute | solution.py:434
  406.8 47.5 %collective-permute-start.61 = (bf16[2,192,384]{2,1,0:T(8,128)(2,1)}, bf16[2,192,384]{2,1,0:T(8,128)(2,1)}, u32[]{:S(2)}, u32[]{:S(2)}) collective-permute-start(bf16[2,192,384]{2,1,0:T(8,128)(2,1)} %get-tuple-element.103), channel_id=1, source_target_pairs={{0,16},{4,20},{8,24},{12,28},{16,0},{20,4},{24,8},{28,12},{1,17},{... | collective-permute-start | bytes 884744 | tf_op jit(solution)/shard_map/ppermute | solution.py:430
  407.7 48.9 %collective-permute-start.66 = (bf16[2,192,384]{2,1,0:T(8,128)(2,1)}, bf16[2,192,384]{2,1,0:T(8,128)(2,1)}, u32[]{:S(2)}, u32[]{:S(2)}) collective-permute-start(bf16[2,192,384]{2,1,0:T(8,128)(2,1)} %get-tuple-element.108), channel_id=1, source_target_pairs={{0,8},{4,12},{8,0},{12,4},{16,24},{20,28},{24,16},{28,20},{1,9},{5... | collective-permute-start | bytes 884744 | tf_op jit(solution)/shard_map/ppermute | solution.py:430
  459.7 36.2 %collective-permute-start.48 = (bf16[4,2,256,256]{3,2,1,0:T(8,128)(2,1)S(1)}, bf16[4,2,256,256]{3,2,1,0:T(8,128)(2,1)S(1)}, u32[]{:S(2)}, u32[]{:S(2)}) collective-permute-start(bf16[4,2,256,256]{3,2,1,0:T(8,128)(2,1)S(1)} %pad_maximum_fusion.4), channel_id=1, source_target_pairs={{1,0},{2,1},{3,2},{5,4},{6,5},{7,6},{9,8},{10,9},{11,10},{13,12},{... | collective-permute-start | bytes 3145736 | tf_op jit(solution)/shard_map/ppermute | solution.py:442
  (116 other events, 1575.8 us)
